TPU v7x, 256 devices: a whole 4x4x8 slice. The times are simulated.
256 devices in a mesh: layer: 4 (over x), row: 8 (over y, core), col: 8 (over z).
Axes of the slice: x: 4, y: 4, z: 8, core: 2. Of those that a mesh axis runs over, the one named last changes fastest.
Arguments:
- cols: int32 [512, 16], P(('row', 'col'), 'layer'), may hold values from -1 to 511, as said below
- vals: bfloat16 [512, 16, 256, 256], P(('row', 'col'), 'layer'), as said below
- outcols: int32 [512, 4], P(('row', 'col')), may hold values from -1 to 511, as said below
Outputs:
- purified: bfloat16 [512, 4, 256, 256], P(('row', 'col'), 'layer')
Inputs may be any that keep to these rules, and one draw needn't show every extreme that they name: `cols`: slots 4 * l to 4 * l + 3 of block row i hold distinct block columns k with k mod 4 = l and |k - i| <= 6, or -1. Column i is always listed in row i, and k is listed in row i exactly when i is listed in row k. vals[i, s] is block (i, cols[i, s]) of a symmetric matrix: the block listed at (k, i) is the transpose of the one at (i, k). Slots holding -1 hold zeros. `outcols`: block row i lists distinct block columns j with i <= j <= i + 12, always i itself, or -1.
All inputs are finite; a program needn't handle non-finite values.
Results may differ from a plain program's by a relative error of at most 0.0085.
Values may be sent and summed in bfloat16 or wider, within the bound.
No kernel may reach another device: no remote copies, remote signals or barrier semaphores. Data moves between devices by JAX's collectives and lax.ppermute only.
A program may use at most 64 MiB of HBM per device.

v0:
```python
import jax
import jax.numpy as jnp
from jax import lax
from jax.sharding import PartitionSpec as P

W = 6


def passed_along(value, axis, by):
    peers = lax.axis_size(axis)
    pairs = [(i, i + by) for i in range(peers) if 0 <= i + by < peers]
    return lax.ppermute(value, axis, pairs)


def per_device(cols, vals, outcols):
    rows = vals.shape[0]
    need = 2 * W
    hops = -(-need // rows)
    blocks_list = [vals]
    column_list = [cols]
    for hop in range(1, hops + 1):
        count = min(rows, need - (hop - 1) * rows)
        got_blocks, got_cols = passed_along((vals[:count], cols[:count]), ("row", "col"), -hop)
        blocks_list.append(got_blocks)
        column_list.append(got_cols)
    extended = jnp.concatenate(blocks_list, axis=0)
    extended_cols = jnp.concatenate(column_list, axis=0)
    offset_rows = lax.axis_index(("row", "col")) * rows

    def one_row(inputs):
        left, left_cols, targets = inputs
        where = jnp.clip(targets - offset_rows, 0, extended_cols.shape[0] - 1)
        right = extended[where]
        right_cols = extended_cols[where]
        hits = (
            (left_cols[None, :, None] == right_cols[:, None, :]) & (left_cols[None, :, None] >= 0)
        ).astype(jnp.bfloat16)
        moved = jnp.einsum(
            "ost,otab->osab", hits, right, preferred_element_type=jnp.float32
        ).astype(jnp.bfloat16)
        product = jnp.einsum("sab,oscb->oac", left, moved, preferred_element_type=jnp.float32)
        owned = (left_cols[None, :] == targets[:, None]).astype(jnp.bfloat16)
        twice = 2.0 * jnp.einsum("os,sab->oab", owned, left, preferred_element_type=jnp.float32)
        return jnp.where(targets[:, None, None] >= 0, twice - product, jnp.float32(0.0))

    partials = lax.map(one_row, (vals, cols, outcols))
    total = lax.psum(partials.astype(jnp.bfloat16), "layer").astype(jnp.float32)
    share = outcols.shape[1] // lax.axis_size("layer")
    mine = lax.dynamic_slice_in_dim(total, lax.axis_index("layer") * share, share, 1)
    return mine.astype(jnp.bfloat16)


def solution(mesh):
    in_specs = (
        P(("row", "col"), "layer"),
        P(("row", "col"), "layer", None, None),
        P(("row", "col"), None),
    )
    out_specs = P(("row", "col"), "layer", None, None)
    return jax.shard_map(
        per_device, mesh=mesh, in_specs=in_specs, out_specs=out_specs, check_vma=False
    )
```

profile of v0, /device:TPU:1, one launch (start us, length us, event | category | flops | bytes accessed | tf_op | source)
XLA Modules:
  0.0 402.7 jit_solution(4357979554235664735)
XLA Ops:
  6.5 9.0 %collective-permute-start.2 = (bf16[8,4,256,256]{3,2,1,0:T(8,128)(2,1)}, bf16[8,4,256,256]{3,2,1,0:T(8,128)(2,1)}, u32[]{:S(2)}, u32[]{:S(2)}) collective-permute-start(bf16[8,4,256,256]{3,2,1,0:T(8,128)(2,1)} %param.6), channel_id=1, source_target_pairs={{1,0},{2,1},{3,2},{4,3},{5,4},{6,5},{7,6},{8,7},{9,8},{10,9},{11,1... | collective-permute-start | bytes 12582920 | tf_op jit(solution)/shard_map/ppermute | solution.py:12
  15.5 3.1 slice.7
  18.7 3.3 collective-permute-start.3
  22.0 2.9 collective-permute-start
  25.0 1.9 collective-permute-start.1
  27.1 165.7 %collective-permute-done.1 = s32[4,4]{0,1:T(4,128)S(1)} collective-permute-done((s32[4,4]{0,1:T(4,128)S(1)}, s32[4,4]{0,1:T(4,128)S(1)}, u32[]{:S(2)}, u32[]{:S(2)}) %collective-permute-start.1) | collective-permute-done | bytes 96 | tf_op jit(solution)/shard_map/ppermute | solution.py:12
  193.0 8.8 %pad_maximum_fusion = bf16[20,4,256,256]{3,2,1,0:T(8,128)(2,1)} fusion(bf16[4,4,256,256]{3,2,1,0:T(8,128)(2,1)S(1)} %collective-permute-done.3, bf16[8,4,256,256]{3,2,1,0:T(8,128)(2,1)} %collective-permute-done.2, bf16[8,4,256,256]{3,2,1,0:T(8,128)(2,1)} %param.6), kind=kLoop, calls=%fused_computation.35 | loop fusion | flops 10485760 | bytes 20971520 | tf_op jit(solution)/shard_map/concatenate | solution.py:26
  201.8 90.1 %while.10 = (s32[]{:T(128)}, bf16[8,4,256,256]{3,2,1,0:T(8,128)(2,1)}, s32[8,4]{1,0:T(8,128)S(1)}, s32[8,4]{1,0:T(8,128)S(1)}, bf16[8,4,256,256]{3,2,1,0:T(8,128...) while((s32[]{:T(128)}, bf16[8,4,256,256]{3,2,1,0:T(8,128)(2,1)}, ...), condition=%wide.region_1.2_spmd, body=%wide.region_0.1_spmd.sunk | while | flops 548144256 | bytes 19403772 | solution.py:46
  201.8 4.7 %gather_fusion = bf16[4,4,256,256]{3,2,1,0:T(8,128)(2,1)S(1)} fusion(bf16[20,4,256,256]{3,2,1,0:T(8,128)(2,1)} %get-tuple-element.168, s32[1024]{0:T(1024)S(1)} %pad_clamp_fusion.2), kind=kCustom, calls=%fused_computation.1.clone.1 | custom fusion | bytes 4194320 | tf_op jit(solution)/shard_map/while/body/eval_jaxpr/gather | solution.py:33
  213.1 4.7 %gather_fusion = bf16[4,4,256,256]{3,2,1,0:T(8,128)(2,1)S(1)} fusion(bf16[20,4,256,256]{3,2,1,0:T(8,128)(2,1)} %get-tuple-element.168, s32[1024]{0:T(1024)S(1)} %pad_clamp_fusion.2), kind=kCustom, calls=%fused_computation.1.clone.1 | custom fusion | bytes 4194320 | tf_op jit(solution)/shard_map/while/body/eval_jaxpr/gather | solution.py:33
  218.3 1.8 fusion.37
  224.3 4.7 %gather_fusion = bf16[4,4,256,256]{3,2,1,0:T(8,128)(2,1)S(1)} fusion(bf16[20,4,256,256]{3,2,1,0:T(8,128)(2,1)} %get-tuple-element.168, s32[1024]{0:T(1024)S(1)} %pad_clamp_fusion.2), kind=kCustom, calls=%fused_computation.1.clone.1 | custom fusion | bytes 4194320 | tf_op jit(solution)/shard_map/while/body/eval_jaxpr/gather | solution.py:33
  229.6 1.8 fusion.37
  235.6 4.7 %gather_fusion = bf16[4,4,256,256]{3,2,1,0:T(8,128)(2,1)S(1)} fusion(bf16[20,4,256,256]{3,2,1,0:T(8,128)(2,1)} %get-tuple-element.168, s32[1024]{0:T(1024)S(1)} %pad_clamp_fusion.2), kind=kCustom, calls=%fused_computation.1.clone.1 | custom fusion | bytes 4194320 | tf_op jit(solution)/shard_map/while/body/eval_jaxpr/gather | solution.py:33
  240.8 1.8 fusion.37
  246.9 4.7 %gather_fusion = bf16[4,4,256,256]{3,2,1,0:T(8,128)(2,1)S(1)} fusion(bf16[20,4,256,256]{3,2,1,0:T(8,128)(2,1)} %get-tuple-element.168, s32[1024]{0:T(1024)S(1)} %pad_clamp_fusion.2), kind=kCustom, calls=%fused_computation.1.clone.1 | custom fusion | bytes 4194320 | tf_op jit(solution)/shard_map/while/body/eval_jaxpr/gather | solution.py:33
  252.1 1.8 fusion.37
  258.1 4.7 %gather_fusion = bf16[4,4,256,256]{3,2,1,0:T(8,128)(2,1)S(1)} fusion(bf16[20,4,256,256]{3,2,1,0:T(8,128)(2,1)} %get-tuple-element.168, s32[1024]{0:T(1024)S(1)} %pad_clamp_fusion.2), kind=kCustom, calls=%fused_computation.1.clone.1 | custom fusion | bytes 4194320 | tf_op jit(solution)/shard_map/while/body/eval_jaxpr/gather | solution.py:33
  263.4 1.8 fusion.37
  269.4 4.7 %gather_fusion = bf16[4,4,256,256]{3,2,1,0:T(8,128)(2,1)S(1)} fusion(bf16[20,4,256,256]{3,2,1,0:T(8,128)(2,1)} %get-tuple-element.168, s32[1024]{0:T(1024)S(1)} %pad_clamp_fusion.2), kind=kCustom, calls=%fused_computation.1.clone.1 | custom fusion | bytes 4194320 | tf_op jit(solution)/shard_map/while/body/eval_jaxpr/gather | solution.py:33
  280.7 4.7 %gather_fusion = bf16[4,4,256,256]{3,2,1,0:T(8,128)(2,1)S(1)} fusion(bf16[20,4,256,256]{3,2,1,0:T(8,128)(2,1)} %get-tuple-element.168, s32[1024]{0:T(1024)S(1)} %pad_clamp_fusion.2), kind=kCustom, calls=%fused_computation.1.clone.1 | custom fusion | bytes 4194320 | tf_op jit(solution)/shard_map/while/body/eval_jaxpr/gather | solution.py:33
  285.9 1.8 fusion.37
  291.9 101.7 %all-reduce.2.cloned.1.call-done = bf16[8,4,256,256]{3,2,1,0:T(8,128)(2,1)} async-done(((bf16[8,4,256,256]{3,2,1,0:T(8,128)(2,1)}), bf16[8,4,256,256]{3,2,1,0:T(8,128)(2,1)}) %all-reduce.2.cloned.1.call-update) | async-done | bytes 4194320 | tf_op jit(solution)/shard_map/psum | solution.py:47
  393.6 2.3 convert_convert_fusion
  (96 shorter events, 42.1 us)
Async XLA Ops:
  6.5 15.5 %copy-start = (s32[8,4]{0,1:T(4,128)S(1)}, s32[8,4]{0,1:T(4,128)}, u32[]{:S(2)}) copy-start(s32[8,4]{0,1:T(4,128)} %param.5) | copy-start | bytes 388
  6.5 20.5 %copy-start.1 = (s32[8,4]{0,1:T(4,128)S(1)}, s32[8,4]{0,1:T(4,128)}, u32[]{:S(2)}) copy-start(s32[8,4]{0,1:T(4,128)} %param.7) | copy-start | bytes 388
  6.5 387.0 %all-reduce.2.cloned.1.call-start = ((), (), s32[]{:S(2)}) async-start(), calls=%async_computation | async-start | bytes 8388608 | tf_op jit(solution)/shard_map/psum | solution.py:47
  6.5 186.4 %collective-permute-start.2 = (bf16[8,4,256,256]{3,2,1,0:T(8,128)(2,1)}, bf16[8,4,256,256]{3,2,1,0:T(8,128)(2,1)}, u32[]{:S(2)}, u32[]{:S(2)}) collective-permute-start(bf16[8,4,256,256]{3,2,1,0:T(8,128)(2,1)} %param.6), channel_id=1, source_target_pairs={{1,0},{2,1},{3,2},{4,3},{5,4},{6,5},{7,6},{8,7},{9,8},{10,9},{11,1... | collective-permute-start | bytes 12582920 | tf_op jit(solution)/shard_map/ppermute | solution.py:12
  18.7 174.3 %collective-permute-start.3 = (bf16[4,4,256,256]{3,2,1,0:T(8,128)(2,1)}, bf16[4,4,256,256]{3,2,1,0:T(8,128)(2,1)S(1)}, u32[]{:S(2)}, u32[]{:S(2)}) collective-permute-start(bf16[4,4,256,256]{3,2,1,0:T(8,128)(2,1)} %slice.7), channel_id=1, source_target_pairs={{2,0},{3,1},{4,2},{5,3},{6,4},{7,5},{8,6},{9,7},{10,8},{11,9},{12,... | collective-permute-start | bytes 6291464 | tf_op jit(solution)/shard_map/ppermute | solution.py:12
  22.0 170.8 %collective-permute-start = (s32[8,4]{0,1:T(4,128)S(1)}, s32[8,4]{0,1:T(4,128)S(1)}, u32[]{:S(2)}, u32[]{:S(2)}) collective-permute-start(s32[8,4]{0,1:T(4,128)S(1)} %copy-done), channel_id=1, source_target_pairs={{1,0},{2,1},{3,2},{4,3},{5,4},{6,5},{7,6},{8,7},{9,8},{10,9},{11,1... | collective-permute-start | bytes 392 | tf_op jit(solution)/shard_map/ppermute | solution.py:12
  25.0 167.8 %collective-permute-start.1 = (s32[4,4]{0,1:T(4,128)S(1)}, s32[4,4]{0,1:T(4,128)S(1)}, u32[]{:S(2)}, u32[]{:S(2)}) collective-permute-start(s32[4,4]{0,1:T(4,128)S(1)} %bitcast.54), channel_id=1, source_target_pairs={{2,0},{3,1},{4,2},{5,3},{6,4},{7,5},{8,6},{9,7},{10,8},{11,9},{12,... | collective-permute-start | bytes 200 | tf_op jit(solution)/shard_map/ppermute | solution.py:12
Sparse Core Ops, SparseCore 0:
  292.0 101.5 all-reduce.1
where the time goes:
time: 404 us; the launch traced here: 403 us
  waiting for transfers between devices  267 us (66%)
  local copies, waits for them, and re-layouts  67.3 us (17%)
  matrix products  25.5 us (6%)
  starting transfers between devices  17.2 us (4%)
  between operations  13.5 us (3%)
  other arithmetic  11.4 us (3%)
    ppermute x4, waiting for transfers between devices, passed_along(): return lax.ppermute(value, axis, pairs)  166 us
    psum x1, waiting for transfers between devices, per_device(): total = lax.psum(partials.astype(jnp.bfloat16), 'layer').astype(jnp.float32)  102 us
    gather x8, local copies, waits for them, and re-layouts, one_row(): right = extended[where]  37.3 us
    ppermute x4, starting transfers between devices, passed_along(): return lax.ppermute(value, axis, pairs)  17.2 us
    dot_general x8, matrix products, one_row(): jnp.einsum('ost,otab->osab', hits, right, preferred_element_type=jnp.floa...  14.1 us
    dynamic_slice x16, local copies, waits for them, and re-layouts, per_device(): partials = lax.map(one_row, (vals, cols, outcols))  11.9 us
    concatenate x1, other arithmetic, per_device(): extended = jnp.concatenate(blocks_list, axis=0)  8.8 us
  transfers between devices with their start and end apart: 5, of which 2 were waited for; matrix products, arithmetic and copies ran while one was open for 1% of the time, Pallas kernels for 0%

commit v1 on v0

v1 whole, which is shorter than its diff:
```python
import functools

import jax
import jax.numpy as jnp
from jax import lax
from jax.experimental import pallas as pl
from jax.experimental.pallas import tpu as pltpu
from jax.sharding import PartitionSpec as P

ROWS = ("row", "col")
B = 256
BF = jnp.bfloat16
F32 = jnp.float32
SM = pl.BlockSpec(memory_space=pltpu.SMEM)
VM = pl.BlockSpec(memory_space=pltpu.VMEM)
ANY = pl.BlockSpec(memory_space=pl.ANY)

OWN, A1, A2, B1, B2 = 0, 32, 39, 45, 53
TWICE, LEFT, LAYER = 128, 160, 176


def shifted(value, axis, by, wrap=True):
    n = lax.axis_size(axis)
    pairs = [(i, (i + by) % n) for i in range(n) if wrap or 0 <= i + by < n]
    return lax.ppermute(value, axis, pairs)


def first_col(row, layer):
    return row - 6 + ((layer - row + 6) & 3)


def b_first(layer):
    return jnp.where(layer < 2, layer + 4, layer)


def pack_kernel(items, place, cols_t, vals, *rest):
    outs, sems = rest[:-1], rest[-1]
    layer = place[0]
    base = place[1]
    copies = []
    for kind, out, pos, where in items:
        if kind == "a":
            m, t = where
            if t == 3:
                m = (layer + 2) & 3
            row = 4 + m
            col = first_col(row, layer) + 4 * t
        else:
            k1 = b_first(layer)
            low = where < k1 - 1
            row = jnp.where(low, where, jnp.minimum(where - (k1 - 1), k1 + 2))
            col = jnp.where(low, k1, k1 + 4) - 8
        hit = jnp.int32(-1)
        empty = jnp.int32(0)
        for s in range(4):
            c = cols_t[s, row]
            hit = jnp.where(c == base + col, s, hit)
            empty = jnp.where(c < 0, s, empty)
        slot = jnp.where(hit >= 0, hit, empty)
        copy = pltpu.make_async_copy(vals.at[row, slot], outs[out].at[pos], sems.at[len(copies)])
        copy.start()
        copies.append(copy)
    for copy in copies:
        copy.wait()


def pack(place, cols_t, vals, items, sizes, name):
    return pl.pallas_call(
        functools.partial(pack_kernel, items),
        out_shape=[jax.ShapeDtypeStruct((n, B, B), BF) for n in sizes],
        in_specs=[SM, SM, ANY],
        out_specs=[VM] * len(sizes),
        scratch_shapes=[pltpu.SemaphoreType.DMA((len(items),))],
        cost_estimate=pl.CostEstimate(
            flops=0, bytes_accessed=len(items) * 2 * B * B * 2, transcendentals=0
        ),
        name=name,
    )(place, cols_t, vals)


def tables(layer, base, cols, outcols, outcols_h):
    rows = jnp.arange(8, dtype=jnp.int32) - 4
    out = jnp.concatenate([outcols_h[4:], outcols[:4]])
    listed = out >= 0
    row_base = jnp.where((rows < 0) & (base == 0), 64 * 8, base)[:, None]
    i = rows[:, None]
    j = jnp.clip(out - row_base, i, i + 12)
    left = first_col(i, layer)
    k = left[:, :, None] + 4 * jnp.arange(4, dtype=jnp.int32)
    ok = listed[:, :, None] & (k >= j[:, :, None] - 6) & (k <= i[:, :, None] + 6)
    jj = j[:, :, None]
    t = jnp.clip((k - first_col(jj, layer)) >> 2, 0, 3)
    in_a = jnp.where(t == 3, A1 + 6, jnp.where(jj >= -2, A1, A2) + 3 * ((-jj - 1) & 1) + t)
    k1 = b_first(layer)
    in_b = jnp.clip(B1 + jj - 8 + jnp.where(k == k1, 0, k1 - 1), B1, B2 + 3)
    slots = jnp.arange(32, dtype=jnp.int32)
    flat = cols.reshape(32)

    def own(row, col):
        here = (slots >> 2) == row[..., None]
        hit = here & (flat == col[..., None] + base)
        free = here & (flat < 0)
        best = jnp.max(jnp.where(hit, slots + 64, jnp.where(free, slots, -1)), axis=-1)
        return jnp.clip(best & 63, 0, 31)

    in_own = own(jnp.broadcast_to(jj, k.shape[:1] + (4, 4)), jnp.broadcast_to(k, (8, 4, 4)))
    right = jnp.where(jj < 0, in_a, jnp.where(jj < 8, in_own, in_b))
    right = jnp.where(ok, right, -1)
    twice = jnp.where(
        listed & ((j & 3) == layer) & (j <= i + 6), jnp.clip((j - left) >> 2, 0, 3), -1
    )
    k_own = k[4:, 0]
    lefts = own(jnp.broadcast_to(i[4:], (4, 4)), k_own)
    parts = [right.reshape(128), twice.reshape(32), lefts.reshape(16), layer[None]]
    return jnp.concatenate(parts).astype(jnp.int32)


def product_kernel(chunk, shifts, table, vals, *rest):
    halo = rest[: 2 * chunk]
    n_out = len(shifts)
    outs, (bbuf, sem) = rest[2 * chunk : 2 * chunk + n_out], rest[2 * chunk + n_out :]
    a_parts, b_parts = halo[:chunk], halo[chunk:]
    layer = table[LAYER]

    def table_row(r):
        return jnp.where(r < 2, 3 - r - 2 * (chunk - 1), 2 + r + 2 * (chunk - 1))

    def right(r, s, t):
        o = (layer + shifts[s]) & 3
        return table[(table_row(r) * 4 + o) * 4 + t]

    pieces = [(OWN, 32, vals), (A1, 7, a_parts[0])]
    if chunk == 2:
        pieces += [(A2, 6, a_parts[1])]
    pieces += [(B1, 8, b_parts[0])]
    if chunk == 2:
        pieces += [(B2, 4, b_parts[1])]

    def issue(r, carry):
        for s in range(n_out):
            for t in range(4):
                b = right(r, s, t)
                dst = bbuf.at[r * n_out + s, t]
                dsem = sem.at[r * n_out + s, t]

                @pl.when(b < 0)
                def _():
                    dst[...] = jnp.zeros((B, B), BF)

                for start, size, ref in pieces:

                    @pl.when((b >= start) & (b < start + size))
                    def _():
                        pltpu.make_async_copy(ref.at[b - start], dst, dsem).start()

        return carry

    lax.fori_loop(0, 4, issue, 0)

    def compute(halo_rows, r, carry):
        lefts = []
        for t in range(4):
            if not halo_rows:
                lefts.append(vals[table[LEFT + (r - 2 + 2 * (chunk - 1)) * 4 + t]])
            elif t == 3:
                lefts.append(a_parts[0][6])
            else:
                lefts.append(a_parts[chunk - 1][3 * r + t])
        for s in range(n_out):
            for t in range(4):

                @pl.when(right(r, s, t) >= 0)
                def _():
                    pltpu.make_async_copy(
                        vals.at[0], bbuf.at[r * n_out + s, t], sem.at[r * n_out + s, t]
                    ).wait()

            acc = jnp.zeros((B, B), F32)
            for t in range(4):
                acc += lax.dot_general(
                    lefts[t],
                    bbuf[r * n_out + s, t],
                    (((1,), (1,)), ((), ())),
                    preferred_element_type=F32,
                )
            outs[s][r] = (-acc).astype(outs[s].dtype)
            o = (layer + shifts[s]) & 3
            own_t = table[TWICE + table_row(r) * 4 + o]
            for t in range(4):

                @pl.when(own_t == t)
                def _():
                    outs[s][r] = (2.0 * lefts[t].astype(F32) - acc).astype(outs[s].dtype)

        return carry

    lax.fori_loop(0, 2, functools.partial(compute, True), 0)
    lax.fori_loop(2, 4, functools.partial(compute, False), 0)


def products(table, vals, a_parts, b_parts, shifts, dtypes, name):
    n, n_out = 4, len(shifts)
    big = (vals, *a_parts, *b_parts)
    return pl.pallas_call(
        functools.partial(product_kernel, len(a_parts), shifts),
        out_shape=[jax.ShapeDtypeStruct((n, B, B), d) for d in dtypes],
        in_specs=[SM] + [VM] * len(big),
        out_specs=[VM] * n_out,
        scratch_shapes=[
            pltpu.VMEM((n * n_out, 4, B, B), BF),
            pltpu.SemaphoreType.DMA((n * n_out, 4)),
        ],
        compiler_params=pltpu.CompilerParams(vmem_limit_bytes=24 << 20),
        cost_estimate=pl.CostEstimate(
            flops=2 * 4 * n * n_out * B**3,
            bytes_accessed=n * n_out * 8 * B * B * 2,
            transcendentals=0,
        ),
        name=name,
    )(table, *big)


def added(whole, part, first):
    half = whole.shape[0] // 2
    a, b = whole[:half], whole[half:]
    if first:
        a = (a.astype(F32) + part.astype(F32)).astype(BF)
    else:
        b = (b.astype(F32) + part.astype(F32)).astype(BF)
    return jnp.concatenate([a, b])


def per_device(cols, vals, outcols):
    base = (lax.axis_index(ROWS) * 8).astype(jnp.int32)
    layer = lax.axis_index("layer").astype(jnp.int32)
    place = jnp.stack([layer, base])
    cols_t = cols.T
    first = [("a", 0, p, (3, p)) for p in range(3)]
    first += [("a", 0, 3 + p, (2, p)) for p in range(3)] + [("a", 0, 6, (0, 3))]
    first += [("b", 1, p, p) for p in range(8)]
    second = [("a", 2, p, (1, p)) for p in range(3)] + [("a", 2, 3 + p, (0, p)) for p in range(3)]
    second += [("b", 3, p, 8 + p) for p in range(4)]
    outcols_h = shifted(outcols, ROWS, 1)
    a1, b1, a2, b2 = pack(place, cols_t, vals, first + second, (7, 8, 6, 4), "pack")
    b1 = shifted(b1, ROWS, -1, False)
    a1 = shifted(a1, ROWS, 1)
    b2 = shifted(b2, ROWS, -1, False)
    a2 = shifted(a2, ROWS, 1)
    table = tables(layer, base, cols, outcols, outcols_h)
    flat = vals.reshape(32, B, B)

    def far(table, a, b, tag):
        (out,) = products(table, flat, a, b, (2,), (BF,), "far" + tag)
        return shifted(out[:2], "layer", 1), shifted(out[2:], "layer", -1)

    def near(table, a, b, tag):
        return products(table, flat, a, b, (1, 3, 0), (BF, BF, F32), "near" + tag)

    got1 = far(table, (a1,), (b1,), "1")
    up1, down1, own1 = near(table, (a1,), (b1,), "1")
    up1, down1 = added(up1, got1[0], True), added(down1, got1[1], False)
    table2, up1, down1 = lax.optimization_barrier((table, up1, down1))
    up1, down1 = shifted(up1, "layer", 1), shifted(down1, "layer", -1)
    got2 = far(table2, (a1, a2), (b1, b2), "2")
    up2, down2, own2 = near(table2, (a1, a2), (b1, b2), "2")
    one = (own1 + up1.astype(F32) + down1.astype(F32)).astype(BF)
    sent1 = shifted(one[:2], ROWS, -1)
    up2, down2 = added(up2, got2[0], True), added(down2, got2[1], False)
    up2, down2 = shifted(up2, "layer", 1), shifted(down2, "layer", -1)
    two = (own2 + up2.astype(F32) + down2.astype(F32)).astype(BF)
    sent2 = shifted(two[:2], ROWS, -1)
    mine = jnp.concatenate([one[2:], two[2:], sent2[::-1], sent1[::-1]])
    return mine[:, None]


def solution(mesh):
    in_specs = (
        P(ROWS, "layer"),
        P(ROWS, "layer", None, None),
        P(ROWS, None),
    )
    out_specs = P(ROWS, "layer", None, None)
    return jax.shard_map(
        per_device, mesh=mesh, in_specs=in_specs, out_specs=out_specs, check_vma=False
    )
```

time: 404 us -> 123 us (0.30)
  waiting for transfers between devices: 267 us -> 33.5 us
  local copies, waits for them, and re-layouts: 67.3 us -> 3.22 us
  Pallas kernels: 0 us -> 37.2 us
  starting transfers between devices: 17.2 us -> 44.5 us
  matrix products: 25.5 us -> 0 us
  between operations: 13.5 us -> 0.3 us
  other arithmetic: 11.4 us -> 3.72 us
    ppermute x4 -> x15, waiting for transfers between devices: 166 us -> 33.5 us  [shifted(): return lax.ppermute(value, axis, pairs)]
    psum x1 -> x0, waiting for transfers between devices: 102 us -> none  [per_device(): total = lax.psum(partials.astype(jnp.bfloat16), 'layer').astype(jnp.float32)]
    gather x16 -> x0, local copies, waits for them, and re-layouts: 41.8 us -> none  [the longest x8 37.3 us: one_row(): right = extended[where]]
    pallas_call x0 -> x5, Pallas kernels: none -> 37.2 us  [the longest x4 32.5 us: products(): pl.pallas_call(functools.partial(product_kernel, len(a_parts), shifts), o...]
    ppermute x4 -> x15, starting transfers between devices: 17.2 us -> 44.5 us  [shifted(): return lax.ppermute(value, axis, pairs)]
    dot_general x24 -> x0, matrix products: 25.5 us -> none  [the longest x8 14.1 us: one_row(): jnp.einsum('ost,otab->osab', hits, right, preferred_element_type=jnp.floa...]
    dynamic_slice x16 -> x0, local copies, waits for them, and re-layouts: 11.9 us -> none  [per_device(): partials = lax.map(one_row, (vals, cols, outcols))]
    concatenate x2 -> x5, other arithmetic: 8.88 us -> 0.27 us  [the longest x4 0.2 us: added(): return jnp.concatenate([a, b])]
  transfers between devices with their start and end apart: 5 -> 15, of which waited for: 2 -> 6; matrix products, arithmetic and copies ran while one was open for 1% -> 3% of each run, Pallas kernels for 0% -> 24%
where the time goes in v1:
time: 123 us; the launch traced here: 122 us
  starting transfers between devices  44.5 us (36%)
  Pallas kernels  37.2 us (30%)
  waiting for transfers between devices  33.5 us (27%)
  other arithmetic  3.72 us (3%)
  local copies, waits for them, and re-layouts  3.22 us (3%)
    ppermute x15, starting transfers between devices, shifted(): return lax.ppermute(value, axis, pairs)  44.5 us
    ppermute x15, waiting for transfers between devices, shifted(): return lax.ppermute(value, axis, pairs)  33.5 us
    pallas_call x4, Pallas kernels, products(): pl.pallas_call(functools.partial(product_kernel, len(a_parts), shifts), o...  32.5 us
    pallas_call x1, Pallas kernels, pack(): pl.pallas_call(functools.partial(pack_kernel, items), out_shape=[jax.Shap...  4.62 us
  transfers between devices with their start and end apart: 15, of which 6 were waited for; matrix products, arithmetic and copies ran while one was open for 3% of the time, Pallas kernels for 24%

profile of v1, /device:TPU:1, one launch (start us, length us, event | category | flops | bytes accessed | tf_op | source)
XLA Modules:
  0.0 122.4 jit_solution(2204255288834782337)
XLA Ops:
  0.0 2.5 %collective-permute-start = (s32[8,4]{0,1:T(4,128)}, s32[8,4]{0,1:T(4,128)S(1)}, u32[]{:S(2)}, u32[]{:S(2)}) collective-permute-start(s32[8,4]{0,1:T(4,128)} %param.5), channel_id=1, source_target_pairs={{0,1},{1,2},{2,3},{3,4},{4,5},{5,6},{6,7},{7,8},{8,9},{9,10},{10,1... | collective-permute-start | bytes 392 | tf_op jit(solution)/shard_map/ppermute | solution.py:25
  3.1 4.6 %pack.1 = (bf16[7,256,256]{2,1,0:T(8,128)(2,1)}, bf16[8,256,256]{2,1,0:T(8,128)(2,1)}, bf16[6,256,256]{2,1,0:T(8,128)(2,1)}, bf16[4,256,256]{2,1,0:T(8,128)(2,1)}) custom-call(s32[2]{0:T(128)} %pad_add_fusion.2.place, s32[4,8]{1,0:T(4,128)} %bitcast.15, bf16[8,4,256,256]{3,2,1,0:T(8,128)(2,1)} %vals.1), custom_call_target="tpu_custom_call" | custom-call | bytes 6553600 | tf_op jit(solution)/shard_map/pack/pallas_call | solution.py:68
  7.8 1.7 %collective-permute-start.1 = (bf16[7,256,256]{2,1,0:T(8,128)(2,1)}, bf16[7,256,256]{2,1,0:T(8,128)(2,1)S(1)}, u32[]{:S(2)}, u32[]{:S(2)}) collective-permute-start(bf16[7,256,256]{2,1,0:T(8,128)(2,1)} %get-tuple-element.18), channel_id=1, source_target_pairs={{0,1},{1,2},{2,3},{3,4},{4,5},{5,6},{6,7},{7,8},{8,9},{9,10},{10,1... | collective-permute-start | bytes 2752520 | tf_op jit(solution)/shard_map/ppermute | solution.py:25
  9.5 4.8 %collective-permute-start.2 = (bf16[8,256,256]{2,1,0:T(8,128)(2,1)}, bf16[8,256,256]{2,1,0:T(8,128)(2,1)S(1)}, u32[]{:S(2)}, u32[]{:S(2)}) collective-permute-start(bf16[8,256,256]{2,1,0:T(8,128)(2,1)} %get-tuple-element.19), channel_id=1, source_target_pairs={{1,0},{2,1},{3,2},{4,3},{5,4},{6,5},{7,6},{8,7},{9,8},{10,9},{11,1... | collective-permute-start | bytes 3145736 | tf_op jit(solution)/shard_map/ppermute | solution.py:25
  16.3 17.2 %collective-permute-done.1.rest_0_ = bf16[7,256,256]{2,1,0:T(8,128)(2,1)S(1)} collective-permute-done((bf16[7,256,256]{2,1,0:T(8,128)(2,1)}, bf16[7,256,256]{2,1,0:T(8,128)(2,1)S(1)}, u32[]{:S(2)}, u32[]{:S(2)}) %collective-permute-start.1) | collective-permute-done | bytes 917536 | tf_op jit(solution)/shard_map/ppermute | solution.py:25
  33.5 1.9 %collective-permute-done.2.rest_1_.rest_2_ = bf16[8,256,256]{2,1,0:T(8,128)(2,1)S(1)} collective-permute-done((bf16[8,256,256]{2,1,0:T(8,128)(2,1)}, bf16[8,256,256]{2,1,0:T(8,128)(2,1)S(1)}, u32[]{:S(2)}, u32[]{:S(2)}) %collective-permute-start.2) | collective-permute-done | bytes 1048608 | tf_op jit(solution)/shard_map/ppermute | solution.py:25
  35.4 2.2 %copy-done = bf16[8,4,256,256]{3,2,1,0:T(8,128)(2,1)S(1)} copy-done((bf16[8,4,256,256]{3,2,1,0:T(8,128)(2,1)S(1)}, bf16[8,4,256,256]{3,2,1,0:T(8,128)(2,1)}, u32[]{:S(2)}) %copy-start) | copy-done | bytes 4194328
  37.5 3.3 %far1.1 = bf16[4,256,256]{2,1,0:T(8,128)(2,1)S(1)} custom-call(s32[177]{0:T(256)S(1)} %pad_add_fusion.1.table, bf16[32,256,256]{2,1,0:T(8,128)(2,1)S(1)} %bitcast.11, bf16[7,256,256]{2,1,0:T(8,128)(2,1)S(1)} %collective-permute-done.1.rest_0_, bf16[8,256,256]{2,1,0:T(8,128)(2,1)S(1)} %collective-permute-done.2.rest_1_.rest_2_), custom_call_target="tpu_custom_call" | custom-call | flops 536870912 | bytes 4194304 | tf_op jit(solution)/shard_map/far1/pallas_call | solution.py:204
  40.9 1.6 %collective-permute-start.3 = (bf16[2,256,256]{2,1,0:T(8,128)(2,1)S(1)}, bf16[2,256,256]{2,1,0:T(8,128)(2,1)S(1)}, u32[]{:S(2)}, u32[]{:S(2)}) collective-permute-start(bf16[2,256,256]{2,1,0:T(8,128)(2,1)S(1)} %get-tuple-element.42), channel_id=1, source_target_pairs={{0,64},{64,128},{128,192},{192,0},{1,65},{65,129},{129,193},{193,1... | collective-permute-start | bytes 786440 | tf_op jit(solution)/shard_map/ppermute | solution.py:25
  42.6 3.3 %collective-permute-start.7 = (bf16[6,256,256]{2,1,0:T(8,128)(2,1)S(1)}, bf16[6,256,256]{2,1,0:T(8,128)(2,1)S(1)}, u32[]{:S(2)}, u32[]{:S(2)}) collective-permute-start(bf16[6,256,256]{2,1,0:T(8,128)(2,1)S(1)} %copy-done.3), channel_id=1, source_target_pairs={{0,1},{1,2},{2,3},{3,4},{4,5},{5,6},{6,7},{7,8},{8,9},{9,10},{10,1... | collective-permute-start | bytes 2359304 | tf_op jit(solution)/shard_map/ppermute | solution.py:25
  45.8 2.6 %collective-permute-start.8 = (bf16[4,256,256]{2,1,0:T(8,128)(2,1)S(1)}, bf16[4,256,256]{2,1,0:T(8,128)(2,1)S(1)}, u32[]{:S(2)}, u32[]{:S(2)}) collective-permute-start(bf16[4,256,256]{2,1,0:T(8,128)(2,1)S(1)} %copy-done.4), channel_id=1, source_target_pairs={{1,0},{2,1},{3,2},{4,3},{5,4},{6,5},{7,6},{8,7},{9,8},{10,9},{11,1... | collective-permute-start | bytes 1572872 | tf_op jit(solution)/shard_map/ppermute | solution.py:25
  48.5 12.3 %near1.1 = (bf16[4,256,256]{2,1,0:T(8,128)(2,1)S(1)}, bf16[4,256,256]{2,1,0:T(8,128)(2,1)S(1)}, f32[4,256,256]{2,1,0:T(8,128)S(1)}) custom-call(s32[177]{0:T(256)S(1)} %pad_add_fusion.1.table, bf16[32,256,256]{2,1,0:T(8,128)(2,1)S(1)} %bitcast.12, bf16[7,256,256]{2,1,0:T(8,128)(2,1)S(1)} %collective-permute-done.1.rest_0_, ...), custom_call_target="tpu_custom_call" | custom-call | flops 1610612736 | bytes 12582912 | tf_op jit(solution)/shard_map/near1/pallas_call | solution.py:204
  61.7 6.9 %collective-permute-done.4 = bf16[2,256,256]{2,1,0:T(8,128)(2,1)S(1)} collective-permute-done((bf16[2,256,256]{2,1,0:T(8,128)(2,1)S(1)}, bf16[2,256,256]{2,1,0:T(8,128)(2,1)S(1)}, u32[]{:S(2)}, u32[]{:S(2)}) %collective-permute-start.4) | collective-permute-done | bytes 262176 | tf_op jit(solution)/shard_map/ppermute | solution.py:25
  68.8 3.9 %far2.1 = bf16[4,256,256]{2,1,0:T(8,128)(2,1)S(1)} custom-call(s32[177]{0:T(256)S(1)} %pad_add_fusion.1.table, bf16[32,256,256]{2,1,0:T(8,128)(2,1)S(1)} %bitcast.13, bf16[7,256,256]{2,1,0:T(8,128)(2,1)S(1)} %collective-permute-done.1.rest_0_, bf16[6,256,256]{2,1,0:T(8,128)(2,1)S(1)} %collective-permute-done.7.rest_1_, ...), custom_call_target="tpu_custom_call" | custom-call | flops 536870912 | bytes 4194304 | tf_op jit(solution)/shard_map/far2/pallas_call | solution.py:204
  72.7 0.9 collective-permute-start.11
  73.7 1.5 %collective-permute-start.6 = (bf16[4,256,256]{2,1,0:T(8,128)(2,1)S(1)}, bf16[4,256,256]{2,1,0:T(8,128)(2,1)S(1)}, u32[]{:S(2)}, u32[]{:S(2)}) collective-permute-start(bf16[4,256,256]{2,1,0:T(8,128)(2,1)S(1)} %pad_maximum_fusion.1), channel_id=1, source_target_pairs={{0,192},{64,0},{128,64},{192,128},{1,193},{65,1},{129,65},{193,129... | collective-permute-start | bytes 1572872 | tf_op jit(solution)/shard_map/ppermute | solution.py:25
  75.1 13.0 %near2.1 = (bf16[4,256,256]{2,1,0:T(8,128)(2,1)S(1)}, bf16[4,256,256]{2,1,0:T(8,128)(2,1)S(1)}, f32[4,256,256]{2,1,0:T(8,128)S(1)}) custom-call(s32[177]{0:T(256)S(1)} %pad_add_fusion.1.table, bf16[32,256,256]{2,1,0:T(8,128)(2,1)S(1)} %bitcast.14, bf16[7,256,256]{2,1,0:T(8,128)(2,1)S(1)} %collective-permute-done.1.rest_0_, ...), custom_call_target="tpu_custom_call" | custom-call | flops 1610612736 | bytes 12582912 | tf_op jit(solution)/shard_map/near2/pallas_call | solution.py:204
  88.2 0.8 collective-permute-start.9
  89.1 2.1 %collective-permute-start.12 = (bf16[4,256,256]{2,1,0:T(8,128)(2,1)S(1)}, bf16[4,256,256]{2,1,0:T(8,128)(2,1)S(1)}, u32[]{:S(2)}, u32[]{:S(2)}) collective-permute-start(bf16[4,256,256]{2,1,0:T(8,128)(2,1)S(1)} %pad_maximum_fusion.3), channel_id=1, source_target_pairs={{0,192},{64,0},{128,64},{192,128},{1,193},{65,1},{129,65},{193,129... | collective-permute-start | bytes 1572872 | tf_op jit(solution)/shard_map/ppermute | solution.py:25
  91.1 3.5 %collective-permute-done.9 = bf16[2,256,256]{2,1,0:T(8,128)(2,1)S(1)} collective-permute-done((bf16[2,256,256]{2,1,0:T(8,128)(2,1)S(1)}, bf16[2,256,256]{2,1,0:T(8,128)(2,1)S(1)}, u32[]{:S(2)}, u32[]{:S(2)}) %collective-permute-start.9) | collective-permute-done | bytes 262176 | tf_op jit(solution)/shard_map/ppermute | solution.py:25
  95.2 9.6 %collective-permute-start.14 = (bf16[2,256,256]{2,1,0:T(8,128)(2,1)S(1)}, bf16[2,256,256]{2,1,0:T(8,128)(2,1)S(1)}, u32[]{:S(2)}, u32[]{:S(2)}) collective-permute-start(bf16[2,256,256]{2,1,0:T(8,128)(2,1)S(1)} %get-tuple-element.36), channel_id=1, source_target_pairs={{0,63},{1,0},{2,1},{3,2},{4,3},{5,4},{6,5},{7,6},{8,7},{9,8},{10,9... | collective-permute-start | bytes 786440 | tf_op jit(solution)/shard_map/ppermute | solution.py:25
  105.6 12.3 %collective-permute-start.13 = (bf16[2,256,256]{2,1,0:T(8,128)(2,1)S(1)}, bf16[2,256,256]{2,1,0:T(8,128)(2,1)S(1)}, u32[]{:S(2)}, u32[]{:S(2)}) collective-permute-start(bf16[2,256,256]{2,1,0:T(8,128)(2,1)S(1)} %get-tuple-element.38), channel_id=1, source_target_pairs={{0,63},{1,0},{2,1},{3,2},{4,3},{5,4},{6,5},{7,6},{8,7},{9,8},{10,9... | collective-permute-start | bytes 786440 | tf_op jit(solution)/shard_map/ppermute | solution.py:25
  118.0 3.3 %collective-permute-done.13 = bf16[2,256,256]{2,1,0:T(8,128)(2,1)S(1)} collective-permute-done((bf16[2,256,256]{2,1,0:T(8,128)(2,1)S(1)}, bf16[2,256,256]{2,1,0:T(8,128)(2,1)S(1)}, u32[]{:S(2)}, u32[]{:S(2)}) %collective-permute-start.13) | collective-permute-done | bytes 262176 | tf_op jit(solution)/shard_map/ppermute | solution.py:25
  121.3 1.1 maximum_bitcast_fusion
  (69 shorter events, 5.1 us)
Async XLA Ops:
  0.0 15.1 %copy-start.2 = (s32[8,4]{0,1:T(4,128)S(1)}, s32[8,4]{0,1:T(4,128)}, u32[]{:S(2)}) copy-start(s32[8,4]{0,1:T(4,128)} %param.5) | copy-start | bytes 388
  0.0 14.3 %copy-start.1 = (s32[8,4]{0,1:T(4,128)S(1)}, s32[8,4]{0,1:T(4,128)}, u32[]{:S(2)}) copy-start(s32[8,4]{0,1:T(4,128)} %param.3) | copy-start | bytes 388
  0.0 15.1 %collective-permute-start = (s32[8,4]{0,1:T(4,128)}, s32[8,4]{0,1:T(4,128)S(1)}, u32[]{:S(2)}, u32[]{:S(2)}) collective-permute-start(s32[8,4]{0,1:T(4,128)} %param.5), channel_id=1, source_target_pairs={{0,1},{1,2},{2,3},{3,4},{4,5},{5,6},{6,7},{7,8},{8,9},{9,10},{10,1... | collective-permute-start | bytes 392 | tf_op jit(solution)/shard_map/ppermute | solution.py:25
  7.8 25.7 %collective-permute-start.1 = (bf16[7,256,256]{2,1,0:T(8,128)(2,1)}, bf16[7,256,256]{2,1,0:T(8,128)(2,1)S(1)}, u32[]{:S(2)}, u32[]{:S(2)}) collective-permute-start(bf16[7,256,256]{2,1,0:T(8,128)(2,1)} %get-tuple-element.18), channel_id=1, source_target_pairs={{0,1},{1,2},{2,3},{3,4},{4,5},{5,6},{6,7},{7,8},{8,9},{9,10},{10,1... | collective-permute-start | bytes 2752520 | tf_op jit(solution)/shard_map/ppermute | solution.py:25
  9.5 25.9 %collective-permute-start.2 = (bf16[8,256,256]{2,1,0:T(8,128)(2,1)}, bf16[8,256,256]{2,1,0:T(8,128)(2,1)S(1)}, u32[]{:S(2)}, u32[]{:S(2)}) collective-permute-start(bf16[8,256,256]{2,1,0:T(8,128)(2,1)} %get-tuple-element.19), channel_id=1, source_target_pairs={{1,0},{2,1},{3,2},{4,3},{5,4},{6,5},{7,6},{8,7},{9,8},{10,9},{11,1... | collective-permute-start | bytes 3145736 | tf_op jit(solution)/shard_map/ppermute | solution.py:25
  35.4 2.2 %copy-start = (bf16[8,4,256,256]{3,2,1,0:T(8,128)(2,1)S(1)}, bf16[8,4,256,256]{3,2,1,0:T(8,128)(2,1)}, u32[]{:S(2)}) copy-start(bf16[8,4,256,256]{3,2,1,0:T(8,128)(2,1)} %vals.1) | copy-start | bytes 12582916
  37.5 5.0 %copy-start.3 = (bf16[6,256,256]{2,1,0:T(8,128)(2,1)S(1)}, bf16[6,256,256]{2,1,0:T(8,128)(2,1)}, u32[]{:S(2)}) copy-start(bf16[6,256,256]{2,1,0:T(8,128)(2,1)} %get-tuple-element.26) | copy-start | bytes 2359300
  37.5 8.3 %copy-start.4 = (bf16[4,256,256]{2,1,0:T(8,128)(2,1)S(1)}, bf16[4,256,256]{2,1,0:T(8,128)(2,1)}, u32[]{:S(2)}) copy-start(bf16[4,256,256]{2,1,0:T(8,128)(2,1)} %get-tuple-element.27) | copy-start | bytes 1572868
  40.9 20.6 %collective-permute-start.3 = (bf16[2,256,256]{2,1,0:T(8,128)(2,1)S(1)}, bf16[2,256,256]{2,1,0:T(8,128)(2,1)S(1)}, u32[]{:S(2)}, u32[]{:S(2)}) collective-permute-start(bf16[2,256,256]{2,1,0:T(8,128)(2,1)S(1)} %get-tuple-element.42), channel_id=1, source_target_pairs={{0,64},{64,128},{128,192},{192,0},{1,65},{65,129},{129,193},{193,1... | collective-permute-start | bytes 786440 | tf_op jit(solution)/shard_map/ppermute | solution.py:25
  42.6 26.2 %collective-permute-start.7 = (bf16[6,256,256]{2,1,0:T(8,128)(2,1)S(1)}, bf16[6,256,256]{2,1,0:T(8,128)(2,1)S(1)}, u32[]{:S(2)}, u32[]{:S(2)}) collective-permute-start(bf16[6,256,256]{2,1,0:T(8,128)(2,1)S(1)} %copy-done.3), channel_id=1, source_target_pairs={{0,1},{1,2},{2,3},{3,4},{4,5},{5,6},{6,7},{7,8},{8,9},{9,10},{10,1... | collective-permute-start | bytes 2359304 | tf_op jit(solution)/shard_map/ppermute | solution.py:25
  45.8 22.9 %collective-permute-start.8 = (bf16[4,256,256]{2,1,0:T(8,128)(2,1)S(1)}, bf16[4,256,256]{2,1,0:T(8,128)(2,1)S(1)}, u32[]{:S(2)}, u32[]{:S(2)}) collective-permute-start(bf16[4,256,256]{2,1,0:T(8,128)(2,1)S(1)} %copy-done.4), channel_id=1, source_target_pairs={{1,0},{2,1},{3,2},{4,3},{5,4},{6,5},{7,6},{8,7},{9,8},{10,9},{11,1... | collective-permute-start | bytes 1572872 | tf_op jit(solution)/shard_map/ppermute | solution.py:25
  60.8 7.8 %collective-permute-start.4 = (bf16[2,256,256]{2,1,0:T(8,128)(2,1)S(1)}, bf16[2,256,256]{2,1,0:T(8,128)(2,1)S(1)}, u32[]{:S(2)}, u32[]{:S(2)}) collective-permute-start(bf16[2,256,256]{2,1,0:T(8,128)(2,1)S(1)} %get-tuple-element.41), channel_id=1, source_target_pairs={{0,192},{64,0},{128,64},{192,128},{1,193},{65,1},{129,65},{193,129... | collective-permute-start | bytes 786440 | tf_op jit(solution)/shard_map/ppermute | solution.py:25
  72.7 16.2 %collective-permute-start.11 = (bf16[2,256,256]{2,1,0:T(8,128)(2,1)S(1)}, bf16[2,256,256]{2,1,0:T(8,128)(2,1)S(1)}, u32[]{:S(2)}, u32[]{:S(2)}) collective-permute-start(bf16[2,256,256]{2,1,0:T(8,128)(2,1)S(1)} %get-tuple-element.40), channel_id=1, source_target_pairs={{0,192},{64,0},{128,64},{192,128},{1,193},{65,1},{129,65},{193,129... | collective-permute-start | bytes 786440 | tf_op jit(solution)/shard_map/ppermute | solution.py:25
  73.7 21.2 %collective-permute-start.6 = (bf16[4,256,256]{2,1,0:T(8,128)(2,1)S(1)}, bf16[4,256,256]{2,1,0:T(8,128)(2,1)S(1)}, u32[]{:S(2)}, u32[]{:S(2)}) collective-permute-start(bf16[4,256,256]{2,1,0:T(8,128)(2,1)S(1)} %pad_maximum_fusion.1), channel_id=1, source_target_pairs={{0,192},{64,0},{128,64},{192,128},{1,193},{65,1},{129,65},{193,129... | collective-permute-start | bytes 1572872 | tf_op jit(solution)/shard_map/ppermute | solution.py:25
  75.1 19.8 %collective-permute-start.5 = (bf16[4,256,256]{2,1,0:T(8,128)(2,1)S(1)}, bf16[4,256,256]{2,1,0:T(8,128)(2,1)S(1)}, u32[]{:S(2)}, u32[]{:S(2)}) collective-permute-start(bf16[4,256,256]{2,1,0:T(8,128)(2,1)S(1)} %pad_maximum_fusion), channel_id=1, source_target_pairs={{0,64},{64,128},{128,192},{192,0},{1,65},{65,129},{129,193},{193,1... | collective-permute-start | bytes 1572872 | tf_op jit(solution)/shard_map/ppermute | solution.py:25
  88.2 6.5 %collective-permute-start.9 = (bf16[2,256,256]{2,1,0:T(8,128)(2,1)S(1)}, bf16[2,256,256]{2,1,0:T(8,128)(2,1)S(1)}, u32[]{:S(2)}, u32[]{:S(2)}) collective-permute-start(bf16[2,256,256]{2,1,0:T(8,128)(2,1)S(1)} %get-tuple-element.39), channel_id=1, source_target_pairs={{0,64},{64,128},{128,192},{192,0},{1,65},{65,129},{129,193},{193,1... | collective-permute-start | bytes 786440 | tf_op jit(solution)/shard_map/ppermute | solution.py:25
  89.1 15.7 %collective-permute-start.12 = (bf16[4,256,256]{2,1,0:T(8,128)(2,1)S(1)}, bf16[4,256,256]{2,1,0:T(8,128)(2,1)S(1)}, u32[]{:S(2)}, u32[]{:S(2)}) collective-permute-start(bf16[4,256,256]{2,1,0:T(8,128)(2,1)S(1)} %pad_maximum_fusion.3), channel_id=1, source_target_pairs={{0,192},{64,0},{128,64},{192,128},{1,193},{65,1},{129,65},{193,129... | collective-permute-start | bytes 1572872 | tf_op jit(solution)/shard_map/ppermute | solution.py:25
  94.8 10.6 %collective-permute-start.10 = (bf16[4,256,256]{2,1,0:T(8,128)(2,1)S(1)}, bf16[4,256,256]{2,1,0:T(8,128)(2,1)S(1)}, u32[]{:S(2)}, u32[]{:S(2)}) collective-permute-start(bf16[4,256,256]{2,1,0:T(8,128)(2,1)S(1)} %pad_maximum_fusion.2), channel_id=1, source_target_pairs={{0,64},{64,128},{128,192},{192,0},{1,65},{65,129},{129,193},{193,1... | collective-permute-start | bytes 1572872 | tf_op jit(solution)/shard_map/ppermute | solution.py:25
  95.2 22.8 %collective-permute-start.14 = (bf16[2,256,256]{2,1,0:T(8,128)(2,1)S(1)}, bf16[2,256,256]{2,1,0:T(8,128)(2,1)S(1)}, u32[]{:S(2)}, u32[]{:S(2)}) collective-permute-start(bf16[2,256,256]{2,1,0:T(8,128)(2,1)S(1)} %get-tuple-element.36), channel_id=1, source_target_pairs={{0,63},{1,0},{2,1},{3,2},{4,3},{5,4},{6,5},{7,6},{8,7},{9,8},{10,9... | collective-permute-start | bytes 786440 | tf_op jit(solution)/shard_map/ppermute | solution.py:25
  105.6 15.6 %collective-permute-start.13 = (bf16[2,256,256]{2,1,0:T(8,128)(2,1)S(1)}, bf16[2,256,256]{2,1,0:T(8,128)(2,1)S(1)}, u32[]{:S(2)}, u32[]{:S(2)}) collective-permute-start(bf16[2,256,256]{2,1,0:T(8,128)(2,1)S(1)} %get-tuple-element.38), channel_id=1, source_target_pairs={{0,63},{1,0},{2,1},{3,2},{4,3},{5,4},{6,5},{7,6},{8,7},{9,8},{10,9... | collective-permute-start | bytes 786440 | tf_op jit(solution)/shard_map/ppermute | solution.py:25

commit v2 on v0

v2 whole, which is shorter than its diff:
```python
import functools

import jax
import jax.numpy as jnp
from jax import lax
from jax.experimental import pallas as pl
from jax.experimental.pallas import tpu as pltpu
from jax.sharding import PartitionSpec as P

ROWS = ("row", "col")
B = 256
BF = jnp.bfloat16
F32 = jnp.float32
I32 = jnp.int32
SM = pl.BlockSpec(memory_space=pltpu.SMEM)
VM = pl.BlockSpec(memory_space=pltpu.VMEM)
ANY = pl.BlockSpec(memory_space=pl.ANY)
HBM = pl.BlockSpec(memory_space=pltpu.HBM)

A_PARTS = (7, 5)
B_PARTS = (7, 4)
A0 = 32
B0 = A0 + sum(A_PARTS)
TURN = B0 + sum(B_PARTS)
ZERO = TURN + 2
POOL = ZERO + 1
TWICE, LEFT, OWN, ENTRIES = 64, 80, 112, 144


def shifted(value, axis, by, wrap=True):
    n = lax.axis_size(axis)
    pairs = [(i, (i + by) % n) for i in range(n) if wrap or 0 <= i + by < n]
    return lax.ppermute(value, axis, pairs)


def in_hbm(value):
    return pltpu.with_memory_space_constraint(value, pltpu.HBM)


def here():
    layer = lax.axis_index("layer").astype(I32)
    device = lax.axis_index(ROWS).astype(I32)
    return layer, device


def first_col(row, layer):
    return row - 6 + ((layer - row + 6) & 3)


def b_first(layer):
    return jnp.where(layer < 2, layer + 4, layer)


def a_count(m, layer):
    return 3 + jnp.where(m == ((layer + 2) & 3), 1, 0) - jnp.where(m == layer, 1, 0)


def a_start(m, layer):
    start = jnp.int32(0)
    for above in (3, 2, 1):
        start += jnp.where(m < above, a_count(above, layer), 0)
    return start


def b_turned(layer):
    return layer + jnp.where(layer < 2, 0, b_first(layer) - 1)


def slot_of(cols_t, row, col):
    hit = jnp.int32(-1)
    empty = jnp.int32(0)
    for s in range(4):
        c = cols_t[s, row]
        hit = jnp.where(c == col, s, hit)
        empty = jnp.where(c < 0, s, empty)
    return jnp.where(hit >= 0, hit, empty)


def pack_kernel(cols_hbm, outcols_hbm, vals, *rest):
    outs, (cols_t, outcols_t, sems, ints_sem) = rest[:4], rest[4:]
    ints = [
        pltpu.make_async_copy(cols_hbm, cols_t, ints_sem.at[0]),
        pltpu.make_async_copy(outcols_hbm, outcols_t, ints_sem.at[1]),
    ]
    for copy in ints:
        copy.start()
    for copy in ints:
        copy.wait()
    layer, device = here()
    base = device * 8
    copies = []

    def send(row, col, dst):
        slot = slot_of(cols_t, row, base + col)
        copy = pltpu.make_async_copy(vals.at[row, slot], dst, sems.at[len(copies)])
        copy.start()
        copies.append(copy)

    def a_block(p):
        m = jnp.int32(3)
        t = jnp.int32(p)
        for above in (3, 2, 1):
            past = p >= a_start(above - 1, layer)
            m = jnp.where(past, above - 1, m)
        t = p - a_start(m, layer)
        row = 4 + m
        return row, first_col(row, layer) + 4 * t

    def b_block(p):
        q = p + jnp.where(p >= b_turned(layer), 1, 0)
        k1 = b_first(layer)
        low = q < k1 - 1
        d = jnp.where(low, q, jnp.minimum(q - (k1 - 1), k1 + 2))
        return d, jnp.where(low, k1, k1 + 4) - 8

    p_a = p_b = 0
    for part in range(2):
        for p in range(A_PARTS[part]):
            dst = outs[0].at[pl.ds(p * B, B)] if part == 0 else outs[2].at[p]
            send(*a_block(p_a), dst)
            p_a += 1
        for p in range(B_PARTS[part]):
            send(*b_block(p_b), outs[2 * part + 1].at[p])
            p_b += 1
    line = lax.broadcasted_iota(I32, (16, B), 0)
    listing = jnp.zeros((16, B), F32)
    for m in range(4):
        for o in range(4):
            col = outcols_t[o, 4 + m]
            away = jnp.where(col >= 0, col - base - 4 - m, -1).astype(F32)
            listing = jnp.where(line == m * 4 + o, away, listing)
    outs[0][pl.ds(A_PARTS[0] * B, 16)] = listing.astype(BF)
    for copy in copies:
        copy.wait()


NOTHING = pl.CostEstimate(flops=0, bytes_accessed=0, transcendentals=0)


def pack(cols_t, outcols_t, vals):
    sizes = (A_PARTS[0], B_PARTS[0], A_PARTS[1], B_PARTS[1])
    shapes = [(A_PARTS[0] * B + 16, B)] + [(n, B, B) for n in sizes[1:]]
    return pl.pallas_call(
        pack_kernel,
        out_shape=[jax.ShapeDtypeStruct(shape, BF) for shape in shapes],
        in_specs=[HBM, HBM, HBM],
        out_specs=[VM] * 4,
        scratch_shapes=[
            pltpu.SMEM((4, 8), I32),
            pltpu.SMEM((4, 8), I32),
            pltpu.SemaphoreType.DMA((sum(sizes),)),
            pltpu.SemaphoreType.DMA((2,)),
        ],
        compiler_params=pltpu.CompilerParams(vmem_limit_bytes=4 << 20),
        cost_estimate=NOTHING,
        name="pack",
    )(in_hbm(cols_t), in_hbm(outcols_t), in_hbm(vals))


def left_place(i, t, layer):
    m = i + 4
    place = jnp.where((m == layer) & (t == 2), TURN, A0 + a_start(m, layer) + t)
    return jnp.where(first_col(i, layer) + 4 * t <= i + 6, place, ZERO)


def row_entries(i, away, layer, table, left, right, twice, at):
    first = first_col(i, layer)
    listed = away >= 0
    j = i + jnp.clip(away, 0, 12)
    first_j = first_col(j, layer)
    start_j = A0 + a_start(j + 4, layer)
    k1 = b_first(layer)
    gap = b_turned(layer)
    for t in range(4):
        k = first + 4 * t
        t_j = jnp.clip((k - first_j) >> 2, 0, 3)
        in_a = jnp.where((j + 4 == layer) & (t_j == 2), TURN, start_j + t_j)
        pos = j - 8 + jnp.where(k == k1, 0, k1 - 1)
        in_b = jnp.where(pos == gap, TURN + 1, B0 + pos - jnp.where(pos > gap, 1, 0))
        place = jnp.where(j < 0, in_a, table[OWN + jnp.clip(j, 0, 7) * 4 + t_j])
        place = jnp.clip(jnp.where(j < 8, place, in_b), 0, ZERO)
        ok = listed & (k >= j - 6) & (k <= i + 6)
        right[at * 4 + t] = jnp.where(ok, place, ZERO)
    doubled = listed & ((j & 3) == layer) & (j <= i + 6)
    t_i = jnp.clip((j - first) >> 2, 0, 3)
    twice(at, jnp.where(doubled, left(t_i), ZERO))


def prepare_kernel(cols_t, outcols_t, vals, table, pool, blocks, sem):
    layer, device = here()
    base = device * 8
    copies = [pltpu.make_async_copy(vals.reshape(32, B, B), pool.at[:A0], sem.at[2])]
    for x, (row, col) in enumerate(((layer, layer - 4), (4 + layer, 8 + layer))):
        slot = slot_of(cols_t, row, base + col)
        copies.append(pltpu.make_async_copy(vals.at[row, slot], blocks.at[x], sem.at[x]))
    for copy in copies:
        copy.start()
    pool[ZERO] = jnp.zeros((B, B), BF)

    def own_row(row, carry):
        first = first_col(row, layer)
        for t in range(4):
            place = row * 4 + slot_of(cols_t, row, base + first + 4 * t)
            table[OWN + row * 4 + t] = place
            valid = first + 4 * t <= row + 6

            @pl.when(row < 4)
            def _():
                table[LEFT + 16 + row * 4 + t] = jnp.where(valid, place, ZERO)
                table[LEFT + row * 4 + t] = left_place(row - 4, jnp.int32(t), layer)

        return carry

    lax.fori_loop(0, 8, own_row, 0)

    def one_row(i, carry):
        def left(t):
            return table[LEFT + 16 + i * 4 + t]

        def twice(at, value):
            table[TWICE + at] = value

        for o in range(4):
            col = outcols_t[o, i]
            away = jnp.where(col >= 0, col - base - i, -1)
            row_entries(i, away, layer, table, left, table, twice, i * 4 + o)
        return carry

    lax.fori_loop(0, 4, one_row, 0)
    for copy in copies:
        copy.wait()
    for x in range(2):
        pool[TURN + x] = blocks[x].T


def prepare(cols_t, outcols_t, vals):
    return pl.pallas_call(
        prepare_kernel,
        out_shape=[
            jax.ShapeDtypeStruct((ENTRIES,), I32),
            jax.ShapeDtypeStruct((POOL, B, B), BF),
        ],
        in_specs=[SM, SM, HBM],
        out_specs=[SM, VM],
        scratch_shapes=[pltpu.VMEM((2, B, B), BF), pltpu.SemaphoreType.DMA((3,))],
        compiler_params=pltpu.CompilerParams(vmem_limit_bytes=4 << 20),
        cost_estimate=NOTHING,
        name="prepare",
    )(cols_t, outcols_t, in_hbm(vals))


TARGETS = {(2, 0): (0, 0), (1, 1): (0, 2), (2, 1): (1, 0), (3, 0): (1, 2)}
TARGETS |= {(1, 0): (2, 0), (3, 1): (3, 0), (0, 0): (4, 0), (0, 1): (5, 0)}
SIZES = (4, 4, 2, 2, 2, 2)


def product_kernel(chunk, table, pool_in, listing, b_part, *rest):
    a_parts, rest = rest[: chunk - 1], rest[chunk - 1 :]
    outs, (pool, lines, away, right, twice, sem) = rest[:6], rest[6:]
    layer, _ = here()
    first_rows = A_PARTS[0] * B
    listed = pltpu.make_async_copy(listing.at[pl.ds(first_rows, 16)], lines, sem.at[0])
    listed.start()
    start = B0 + sum(B_PARTS[: chunk - 1])
    pieces = [(b_part, start, B_PARTS[chunk - 1])]
    if chunk == 1:
        pieces += [(listing.at[pl.ds(p * B, B)], A0 + p, 0) for p in range(A_PARTS[0])]
    else:
        pieces += [(a_parts[0], A0 + A_PARTS[0], A_PARTS[1])]
    copies = [
        pltpu.make_async_copy(
            ref, pool.at[start : start + size] if size else pool.at[start], sem.at[1 + x]
        )
        for x, (ref, start, size) in enumerate(pieces)
    ]
    for copy in copies:
        copy.start()
    listed.wait()
    away[...] = lines[:, :128].astype(F32).astype(I32)

    def row_of(above, r):
        return r + 2 * (chunk - 1) if above else -1 - r - 2 * (chunk - 1)

    def below_row(r, carry):
        i = row_of(0, r)

        def left(t):
            return table[LEFT + (i + 4) * 4 + t]

        def store(at, value):
            twice[at] = value

        for o in range(4):
            far = away[(i + 4) * 4 + o, 0]
            row_entries(i, far, layer, table, left, right, store, r * 4 + o)
        return carry

    lax.fori_loop(0, 2, below_row, 0)
    for copy in copies:
        copy.wait()

    def compute(above, r, carry):
        i = row_of(above, r)
        lefts = [table[LEFT + (i + 4) * 4 + t] for t in range(4)]
        for shift in (2, 1, 3, 0):
            o = (layer + shift) & 3
            acc = jnp.zeros((B, B), F32)
            for t in range(4):
                place = table[(i * 4 + o) * 4 + t] if above else right[(r * 4 + o) * 4 + t]
                acc += lax.dot_general(
                    pool[lefts[t]],
                    pool[place],
                    (((1,), (1,)), ((), ())),
                    preferred_element_type=F32,
                )
            own = table[TWICE + i * 4 + o] if above else twice[r * 4 + o]
            factor = jnp.where(own < ZERO, 2.0, 0.0).astype(F32)
            out, start = TARGETS[shift, above]
            outs[out][start + r] = (factor * pool[own].astype(F32) - acc).astype(BF)
        return carry

    lax.fori_loop(0, 2, functools.partial(compute, 0), 0)
    lax.fori_loop(0, 2, functools.partial(compute, 1), 0)


def products(table, pool, halo, chunk, name):
    return pl.pallas_call(
        functools.partial(product_kernel, chunk),
        out_shape=[jax.ShapeDtypeStruct((n, B, B), BF) for n in (*SIZES, POOL)],
        in_specs=[SM, VM] + [ANY] * len(halo),
        out_specs=[VM] * (len(SIZES) + 1),
        scratch_shapes=[
            pltpu.VMEM((16, B), BF),
            pltpu.VMEM((16, 128), I32),
            pltpu.SMEM((32,), I32),
            pltpu.SMEM((8,), I32),
            pltpu.SemaphoreType.DMA((2 + A_PARTS[0],)),
        ],
        input_output_aliases={1: len(SIZES)},
        compiler_params=pltpu.CompilerParams(vmem_limit_bytes=4 << 20),
        cost_estimate=NOTHING,
        name=name,
    )(table, pool, *halo)


def total(*parts):
    return sum(part.astype(F32) for part in parts).astype(BF)


def adds_kernel(a, b, c, d, x, y):
    x[...] = total(a[...], b[:2])
    y[...] = total(c[...], d[:2])


def adds(a, b, c, d, name, cost):
    return pl.pallas_call(
        adds_kernel,
        out_shape=[jax.ShapeDtypeStruct((2, B, B), BF)] * 2,
        in_specs=[VM] * 4,
        out_specs=[VM] * 2,
        compiler_params=pltpu.CompilerParams(vmem_limit_bytes=4 << 20),
        cost_estimate=pl.CostEstimate(flops=0, bytes_accessed=cost, transcendentals=0),
        name=name,
    )(a, b, c, d)


def finish_kernel(sums, copied, *rest):
    n_in = 3 * len(sums) + len(copied)
    parts, (out, block, sem) = rest[:n_in], rest[-3:]
    copies = []

    def send(src, row):
        copy = pltpu.make_async_copy(src, out.at[row], sem.at[len(copies)])
        copy.start()
        copies.append(copy)

    for x, rows in enumerate(copied):
        for r in range(2):
            send(parts[3 * len(sums) + x].at[r], rows[r])
    for x, rows in enumerate(sums):
        own, plus, minus = parts[3 * x : 3 * x + 3]
        for r in range(2):
            block[2 * x + r] = total(own[r], plus[2 + r], minus[r])
            send(block.at[2 * x + r], rows[r])
    for copy in copies:
        copy.wait()


def finish(sums, copied, parts, before, name):
    n = 2 * len(sums) + 2 * len(copied)
    return pl.pallas_call(
        functools.partial(finish_kernel, sums, copied),
        out_shape=jax.ShapeDtypeStruct((8, B, B), BF),
        in_specs=[VM] * len(parts) + [HBM] * len(before),
        out_specs=HBM,
        scratch_shapes=[
            pltpu.VMEM((max(2 * len(sums), 1), B, B), BF),
            pltpu.SemaphoreType.DMA((n,)),
        ],
        input_output_aliases={len(parts): 0} if before else {},
        compiler_params=pltpu.CompilerParams(vmem_limit_bytes=4 << 20),
        cost_estimate=NOTHING,
        name=name,
    )(*parts, *before)


def per_device(cols, vals, outcols):
    both = lax.optimization_barrier
    a1, b1, a2, b2 = pack(cols.T, outcols.T, vals)
    a1 = shifted(a1, ROWS, 1)
    b1 = shifted(b1, ROWS, -1, False)
    a2 = shifted(a2, ROWS, 1)
    b2 = shifted(b2, ROWS, -1, False)
    table, pool = prepare(cols.T, outcols.T, vals)

    out1 = products(table, pool, (a1, b1), 1, "products1")
    plus1, minus1, up_b1, down1, own_b1, own1, pool = out1
    plus1, minus1 = shifted(plus1, "layer", 1), shifted(minus1, "layer", -1)
    out2 = products(table, pool, (a1, b2, a2), 2, "products2")
    plus2, minus2, up_b2, down2, own_b2, own2, pool = out2
    (plus1, minus1), _ = both(((plus1, minus1), own_b2))
    plus2, minus2 = shifted(plus2, "layer", 1), shifted(minus2, "layer", -1)

    def second(plus, minus, up_below, down, own_below, name, cost):
        up_below, down = adds(up_below, plus, down, minus, name, cost)
        up_below = shifted(up_below, "layer", 1)
        down = shifted(down, "layer", -1)
        below = shifted(total(own_below, minus[2:], up_below), ROWS, -1)
        return down, below

    down1, below1 = second(plus1, minus1, up_b1, down1, own_b1, "adds1", 40 << 20)
    plus2, minus2 = both((plus2, minus2))
    down2, below2 = second(plus2, minus2, up_b2, down2, own_b2, "adds2", 0)
    parts = (own1, plus1, down1, own2, plus2, down2, below1)
    mine = finish(((0, 1), (2, 3)), ((7, 6),), parts, (), "finish1")
    mine = finish((), ((5, 4),), (below2,), (mine,), "finish2")
    return mine[:, None]


def solution(mesh):
    in_specs = (
        P(ROWS, "layer"),
        P(ROWS, "layer", None, None),
        P(ROWS, None),
    )
    out_specs = P(ROWS, "layer", None, None)
    return jax.shard_map(
        per_device, mesh=mesh, in_specs=in_specs, out_specs=out_specs, check_vma=False
    )
```

time: 404 us -> 86.1 us (0.21)
  waiting for transfers between devices: 267 us -> 30.7 us
  local copies, waits for them, and re-layouts: 67.3 us -> 1.36 us
  matrix products: 25.5 us -> 0 us
  Pallas kernels: 0 us -> 18.2 us
  starting transfers between devices: 17.2 us -> 34.9 us
  between operations: 13.5 us -> 0.1 us
  other arithmetic: 11.4 us -> 0.2 us
    ppermute x4 -> x14, waiting for transfers between devices: 166 us -> 30.7 us  [shifted(): return lax.ppermute(value, axis, pairs)]
    psum x1 -> x0, waiting for transfers between devices: 102 us -> none  [per_device(): total = lax.psum(partials.astype(jnp.bfloat16), 'layer').astype(jnp.float32)]
    gather x16 -> x0, local copies, waits for them, and re-layouts: 41.8 us -> none  [the longest x8 37.3 us: one_row(): right = extended[where]]
    dot_general x24 -> x0, matrix products: 25.5 us -> none  [the longest x8 14.1 us: one_row(): jnp.einsum('ost,otab->osab', hits, right, preferred_element_type=jnp.floa...]
    pallas_call x0 -> x8, Pallas kernels: none -> 18.2 us  [the longest x2 9.97 us: products(): pl.pallas_call(functools.partial(product_kernel, chunk), out_shape=[jax.S...]
    ppermute x4 -> x14, starting transfers between devices: 17.2 us -> 34.9 us  [shifted(): return lax.ppermute(value, axis, pairs)]
    dynamic_slice x16 -> x0, local copies, waits for them, and re-layouts: 11.9 us -> none  [per_device(): partials = lax.map(one_row, (vals, cols, outcols))]
    concatenate x2 -> x0, other arithmetic: 8.88 us -> none  [the longest x1 8.8 us: per_device(): extended = jnp.concatenate(blocks_list, axis=0)]
  transfers between devices with their start and end apart: 5 -> 14, of which waited for: 2 -> 7; matrix products, arithmetic and copies ran while one was open for 1% -> 0% of each run, Pallas kernels for 0% -> 17%
where the time goes in v2:
time: 86.1 us; the launch traced here: 85.5 us
  starting transfers between devices  34.9 us (41%)
  waiting for transfers between devices  30.7 us (36%)
  Pallas kernels  18.2 us (21%)
  local copies, waits for them, and re-layouts  1.36 us (2%)
    ppermute x14, starting transfers between devices, shifted(): return lax.ppermute(value, axis, pairs)  34.9 us
    ppermute x14, waiting for transfers between devices, shifted(): return lax.ppermute(value, axis, pairs)  30.7 us
    pallas_call x2, Pallas kernels, products(): pl.pallas_call(functools.partial(product_kernel, chunk), out_shape=[jax.S...  9.97 us
    pallas_call x1, Pallas kernels, prepare(): pl.pallas_call(prepare_kernel, out_shape=[jax.ShapeDtypeStruct((ENTRIES,)...  3.43 us
    pallas_call x1, Pallas kernels, pack(): pl.pallas_call(pack_kernel, out_shape=[jax.ShapeDtypeStruct(shape, BF) fo...  2.91 us
  transfers between devices with their start and end apart: 14, of which 7 were waited for; matrix products, arithmetic and copies ran while one was open for 0% of the time, Pallas kernels for 17%

profile of v2, /device:TPU:1, one launch (start us, length us, event | category | flops | bytes accessed | tf_op | source)
XLA Modules:
  0.0 85.5 jit_solution(13272717557431865210)
XLA Ops:
  0.0 2.9 %pack.1 = (bf16[1808,256]{1,0:T(8,128)(2,1)S(1)}, bf16[7,256,256]{2,1,0:T(8,128)(2,1)S(1)}, bf16[5,256,256]{2,1,0:T(8,128)(2,1)S(1)}, bf16[4,256,256]{2,1,0:T(8,128)(2,1)S(1)}) custom-call(s32[4,8]{1,0:T(4,128)} %bitcast.5, s32[4,8]{1,0:T(4,128)} %bitcast.7, bf16[8,4,256,256]{3,2,1,0:T(8,128)(2,1)} %vals.3), custom_call_target="tpu_custom_call" | custom-call | tf_op jit(solution)/shard_map/pack/pallas_call | solution.py:143
  2.9 2.5 %collective-permute-start = (bf16[1808,256]{1,0:T(8,128)(2,1)S(1)}, bf16[1808,256]{1,0:T(8,128)(2,1)S(1)}, u32[]{:S(2)}, u32[]{:S(2)}) collective-permute-start(bf16[1808,256]{1,0:T(8,128)(2,1)S(1)} %get-tuple-element.34), channel_id=1, source_target_pairs={{0,1},{1,2},{2,3},{3,4},{4,5},{5,6},{6,7},{7,8},{8,9},{9,10},{10,1... | collective-permute-start | bytes 2777096 | tf_op jit(solution)/shard_map/ppermute | solution.py:33
  5.5 6.6 %collective-permute-start.1 = (bf16[7,256,256]{2,1,0:T(8,128)(2,1)S(1)}, bf16[7,256,256]{2,1,0:T(8,128)(2,1)S(1)}, u32[]{:S(2)}, u32[]{:S(2)}) collective-permute-start(bf16[7,256,256]{2,1,0:T(8,128)(2,1)S(1)} %get-tuple-element.35), channel_id=1, source_target_pairs={{1,0},{2,1},{3,2},{4,3},{5,4},{6,5},{7,6},{8,7},{9,8},{10,9},{11,1... | collective-permute-start | bytes 2752520 | tf_op jit(solution)/shard_map/ppermute | solution.py:33
  12.1 4.8 %collective-permute-start.2 = (bf16[4,256,256]{2,1,0:T(8,128)(2,1)S(1)}, bf16[4,256,256]{2,1,0:T(8,128)(2,1)S(1)}, u32[]{:S(2)}, u32[]{:S(2)}) collective-permute-start(bf16[4,256,256]{2,1,0:T(8,128)(2,1)S(1)} %get-tuple-element.37), channel_id=1, source_target_pairs={{1,0},{2,1},{3,2},{4,3},{5,4},{6,5},{7,6},{8,7},{9,8},{10,9},{11,1... | collective-permute-start | bytes 1572872 | tf_op jit(solution)/shard_map/ppermute | solution.py:33
  18.3 3.4 %prepare.1 = (s32[144]{0:T(256)S(1)}, bf16[58,256,256]{2,1,0:T(8,128)(2,1)S(1)}) custom-call(s32[4,8]{1,0:T(4,128)S(1)} %bitcast.6, s32[4,8]{1,0:T(4,128)S(1)} %bitcast.8, bf16[8,4,256,256]{3,2,1,0:T(8,128)(2,1)} %vals.3), custom_call_target="tpu_custom_call" | custom-call | tf_op jit(solution)/shard_map/prepare/pallas_call | solution.py:237
  21.8 6.8 %collective-permute-done.1.b_part = bf16[7,256,256]{2,1,0:T(8,128)(2,1)S(1)} collective-permute-done((bf16[7,256,256]{2,1,0:T(8,128)(2,1)S(1)}, bf16[7,256,256]{2,1,0:T(8,128)(2,1)S(1)}, u32[]{:S(2)}, u32[]{:S(2)}) %collective-permute-start.1) | collective-permute-done | bytes 917536 | tf_op jit(solution)/shard_map/ppermute | solution.py:33
  28.6 2.9 %collective-permute-done.listing = bf16[1808,256]{1,0:T(8,128)(2,1)S(1)} collective-permute-done((bf16[1808,256]{1,0:T(8,128)(2,1)S(1)}, bf16[1808,256]{1,0:T(8,128)(2,1)S(1)}, u32[]{:S(2)}, u32[]{:S(2)}) %collective-permute-start) | collective-permute-done | bytes 925728 | tf_op jit(solution)/shard_map/ppermute | solution.py:33
  31.5 5.6 %products1.1 = (bf16[4,256,256]{2,1,0:T(8,128)(2,1)S(1)}, bf16[4,256,256]{2,1,0:T(8,128)(2,1)S(1)}, bf16[2,256,256]{2,1,0:T(8,128)(2,1)S(1)}, bf16[2,256,256]{2,...) custom-call(s32[144]{0:T(256)S(1)} %get-tuple-element.32.table, ...), custom_call_target="tpu_custom_call", output_to_operand_aliasing={{6}: (1, {})} | custom-call | tf_op jit(solution)/shard_map/products1/pallas_call | solution.py:327
  37.0 1.1 %collective-permute-start.8 = (bf16[4,256,256]{2,1,0:T(8,128)(2,1)S(1)}, bf16[4,256,256]{2,1,0:T(8,128)(2,1)S(1)}, u32[]{:S(2)}, u32[]{:S(2)}) collective-permute-start(bf16[4,256,256]{2,1,0:T(8,128)(2,1)S(1)} %get-tuple-element.48), channel_id=1, source_target_pairs={{0,64},{64,128},{128,192},{192,0},{1,65},{65,129},{129,193},{193,1... | collective-permute-start | bytes 1572872 | tf_op jit(solution)/shard_map/ppermute | solution.py:33
  38.2 1.6 %collective-permute-start.9 = (bf16[4,256,256]{2,1,0:T(8,128)(2,1)S(1)}, bf16[4,256,256]{2,1,0:T(8,128)(2,1)S(1)}, u32[]{:S(2)}, u32[]{:S(2)}) collective-permute-start(bf16[4,256,256]{2,1,0:T(8,128)(2,1)S(1)} %get-tuple-element.49), channel_id=1, source_target_pairs={{0,192},{64,0},{128,64},{192,128},{1,193},{65,1},{129,65},{193,129... | collective-permute-start | bytes 1572872 | tf_op jit(solution)/shard_map/ppermute | solution.py:33
  39.8 4.7 %collective-permute-done.3.rest_0_ = bf16[5,256,256]{2,1,0:T(8,128)(2,1)S(1)} collective-permute-done((bf16[5,256,256]{2,1,0:T(8,128)(2,1)S(1)}, bf16[5,256,256]{2,1,0:T(8,128)(2,1)S(1)}, u32[]{:S(2)}, u32[]{:S(2)}) %collective-permute-start.3) | collective-permute-done | bytes 655392 | tf_op jit(solution)/shard_map/ppermute | solution.py:33
  44.5 4.4 %products2.1 = (bf16[4,256,256]{2,1,0:T(8,128)(2,1)S(1)}, bf16[4,256,256]{2,1,0:T(8,128)(2,1)S(1)}, bf16[2,256,256]{2,1,0:T(8,128)(2,1)S(1)}, bf16[2,256,256]{2,...) custom-call(s32[144]{0:T(256)S(1)} %get-tuple-element.32.table, ...), custom_call_target="tpu_custom_call", output_to_operand_aliasing={{6}: (1, {})} | custom-call | tf_op jit(solution)/shard_map/products2/pallas_call | solution.py:327
  48.9 1.3 %collective-permute-start.4 = (bf16[4,256,256]{2,1,0:T(8,128)(2,1)S(1)}, bf16[4,256,256]{2,1,0:T(8,128)(2,1)S(1)}, u32[]{:S(2)}, u32[]{:S(2)}) collective-permute-start(bf16[4,256,256]{2,1,0:T(8,128)(2,1)S(1)} %get-tuple-element.40), channel_id=1, source_target_pairs={{0,64},{64,128},{128,192},{192,0},{1,65},{65,129},{129,193},{193,1... | collective-permute-start | bytes 1572872 | tf_op jit(solution)/shard_map/ppermute | solution.py:33
  50.2 1.5 %collective-permute-start.5 = (bf16[4,256,256]{2,1,0:T(8,128)(2,1)S(1)}, bf16[4,256,256]{2,1,0:T(8,128)(2,1)S(1)}, u32[]{:S(2)}, u32[]{:S(2)}) collective-permute-start(bf16[4,256,256]{2,1,0:T(8,128)(2,1)S(1)} %get-tuple-element.41), channel_id=1, source_target_pairs={{0,192},{64,0},{128,64},{192,128},{1,193},{65,1},{129,65},{193,129... | collective-permute-start | bytes 1572872 | tf_op jit(solution)/shard_map/ppermute | solution.py:33
  52.1 9.5 %collective-permute-done.4.b.rest_4_ = bf16[4,256,256]{2,1,0:T(8,128)(2,1)S(1)} collective-permute-done((bf16[4,256,256]{2,1,0:T(8,128)(2,1)S(1)}, bf16[4,256,256]{2,1,0:T(8,128)(2,1)S(1)}, u32[]{:S(2)}, u32[]{:S(2)}) %collective-permute-start.4) | collective-permute-done | bytes 524320 | tf_op jit(solution)/shard_map/ppermute | solution.py:33
  61.8 1.4 %collective-permute-start.6 = (bf16[2,256,256]{2,1,0:T(8,128)(2,1)S(1)}, bf16[2,256,256]{2,1,0:T(8,128)(2,1)S(1)}, u32[]{:S(2)}, u32[]{:S(2)}) collective-permute-start(bf16[2,256,256]{2,1,0:T(8,128)(2,1)S(1)} %get-tuple-element.46), channel_id=1, source_target_pairs={{0,64},{64,128},{128,192},{192,0},{1,65},{65,129},{129,193},{193,1... | collective-permute-start | bytes 786440 | tf_op jit(solution)/shard_map/ppermute | solution.py:33
  63.2 1.4 %collective-permute-start.11 = (bf16[2,256,256]{2,1,0:T(8,128)(2,1)S(1)}, bf16[2,256,256]{2,1,0:T(8,128)(2,1)S(1)}, u32[]{:S(2)}, u32[]{:S(2)}) collective-permute-start(bf16[2,256,256]{2,1,0:T(8,128)(2,1)S(1)} %get-tuple-element.56), channel_id=1, source_target_pairs={{0,192},{64,0},{128,64},{192,128},{1,193},{65,1},{129,65},{193,129... | collective-permute-start | bytes 786440 | tf_op jit(solution)/shard_map/ppermute | solution.py:33
  64.5 1.2 %collective-permute-start.10 = (bf16[2,256,256]{2,1,0:T(8,128)(2,1)S(1)}, bf16[2,256,256]{2,1,0:T(8,128)(2,1)S(1)}, u32[]{:S(2)}, u32[]{:S(2)}) collective-permute-start(bf16[2,256,256]{2,1,0:T(8,128)(2,1)S(1)} %get-tuple-element.54), channel_id=1, source_target_pairs={{0,192},{64,0},{128,64},{192,128},{1,193},{65,1},{129,65},{193,129... | collective-permute-start | bytes 786440 | tf_op jit(solution)/shard_map/ppermute | solution.py:33
  65.7 1.6 %collective-permute-done.12 = bf16[2,256,256]{2,1,0:T(8,128)(2,1)S(1)} collective-permute-done((bf16[2,256,256]{2,1,0:T(8,128)(2,1)S(1)}, bf16[2,256,256]{2,1,0:T(8,128)(2,1)S(1)}, u32[]{:S(2)}, u32[]{:S(2)}) %collective-permute-start.12) | collective-permute-done | bytes 262176 | tf_op jit(solution)/shard_map/ppermute | solution.py:33
  67.4 5.7 %collective-permute-start.13 = (bf16[2,256,256]{2,1,0:T(8,128)(2,1)S(1)}, bf16[2,256,256]{2,1,0:T(8,128)(2,1)S(1)}, u32[]{:S(2)}, u32[]{:S(2)}) collective-permute-start(bf16[2,256,256]{2,1,0:T(8,128)(2,1)S(1)} %add_convert_fusion), channel_id=1, source_target_pairs={{0,63},{1,0},{2,1},{3,2},{4,3},{5,4},{6,5},{7,6},{8,7},{9,8},{10,9... | collective-permute-start | bytes 786440 | tf_op jit(solution)/shard_map/ppermute | solution.py:33
  73.2 5.4 %collective-permute-start.7 = (bf16[2,256,256]{2,1,0:T(8,128)(2,1)S(1)}, bf16[2,256,256]{2,1,0:T(8,128)(2,1)S(1)}, u32[]{:S(2)}, u32[]{:S(2)}) collective-permute-start(bf16[2,256,256]{2,1,0:T(8,128)(2,1)S(1)} %add_convert_fusion.1), channel_id=1, source_target_pairs={{0,63},{1,0},{2,1},{3,2},{4,3},{5,4},{6,5},{7,6},{8,7},{9,8},{10,9... | collective-permute-start | bytes 786440 | tf_op jit(solution)/shard_map/ppermute | solution.py:33
  79.1 0.9 %finish1.1.rest_1_ = bf16[8,256,256]{2,1,0:T(8,128)(2,1)} custom-call(bf16[2,256,256]{2,1,0:T(8,128)(2,1)S(1)} %get-tuple-element.47.rest_0_, bf16[4,256,256]{2,1,0:T(8,128)(2,1)S(1)} %collective-permute-done.8.b.rest_1_, bf16[2,256,256]{2,1,0:T(8,128)(2,1)S(1)} %collective-permute-done.10.rest_2_, bf16[2,256,256]{2,1,0:T(8,128)(2,1)S(1)} %get-tuple-element.55.rest_3_, ...), custom_call_target="tpu_custom_call" | custom-call | tf_op jit(solution)/shard_map/finish1/pallas_call | solution.py:391
  80.1 4.7 %collective-permute-done.7.rest_0_ = bf16[2,256,256]{2,1,0:T(8,128)(2,1)S(1)} collective-permute-done((bf16[2,256,256]{2,1,0:T(8,128)(2,1)S(1)}, bf16[2,256,256]{2,1,0:T(8,128)(2,1)S(1)}, u32[]{:S(2)}, u32[]{:S(2)}) %collective-permute-start.7) | collective-permute-done | bytes 262176 | tf_op jit(solution)/shard_map/ppermute | solution.py:33
  84.8 0.7 finish2.1
  (18 shorter events, 2.8 us)
Async XLA Ops:
  2.9 28.6 %collective-permute-start = (bf16[1808,256]{1,0:T(8,128)(2,1)S(1)}, bf16[1808,256]{1,0:T(8,128)(2,1)S(1)}, u32[]{:S(2)}, u32[]{:S(2)}) collective-permute-start(bf16[1808,256]{1,0:T(8,128)(2,1)S(1)} %get-tuple-element.34), channel_id=1, source_target_pairs={{0,1},{1,2},{2,3},{3,4},{4,5},{5,6},{6,7},{7,8},{8,9},{9,10},{10,1... | collective-permute-start | bytes 2777096 | tf_op jit(solution)/shard_map/ppermute | solution.py:33
  5.5 23.1 %collective-permute-start.1 = (bf16[7,256,256]{2,1,0:T(8,128)(2,1)S(1)}, bf16[7,256,256]{2,1,0:T(8,128)(2,1)S(1)}, u32[]{:S(2)}, u32[]{:S(2)}) collective-permute-start(bf16[7,256,256]{2,1,0:T(8,128)(2,1)S(1)} %get-tuple-element.35), channel_id=1, source_target_pairs={{1,0},{2,1},{3,2},{4,3},{5,4},{6,5},{7,6},{8,7},{9,8},{10,9},{11,1... | collective-permute-start | bytes 2752520 | tf_op jit(solution)/shard_map/ppermute | solution.py:33
  12.0 32.5 %collective-permute-start.3 = (bf16[5,256,256]{2,1,0:T(8,128)(2,1)S(1)}, bf16[5,256,256]{2,1,0:T(8,128)(2,1)S(1)}, u32[]{:S(2)}, u32[]{:S(2)}) collective-permute-start(bf16[5,256,256]{2,1,0:T(8,128)(2,1)S(1)} %get-tuple-element.38), channel_id=1, source_target_pairs={{0,1},{1,2},{2,3},{3,4},{4,5},{5,6},{6,7},{7,8},{8,9},{9,10},{10,1... | collective-permute-start | bytes 1966088 | tf_op jit(solution)/shard_map/ppermute | solution.py:33
  12.1 27.7 %collective-permute-start.2 = (bf16[4,256,256]{2,1,0:T(8,128)(2,1)S(1)}, bf16[4,256,256]{2,1,0:T(8,128)(2,1)S(1)}, u32[]{:S(2)}, u32[]{:S(2)}) collective-permute-start(bf16[4,256,256]{2,1,0:T(8,128)(2,1)S(1)} %get-tuple-element.37), channel_id=1, source_target_pairs={{1,0},{2,1},{3,2},{4,3},{5,4},{6,5},{7,6},{8,7},{9,8},{10,9},{11,1... | collective-permute-start | bytes 1572872 | tf_op jit(solution)/shard_map/ppermute | solution.py:33
  17.0 0.7 copy-start
  17.7 0.7 copy-start.1
  37.0 14.7 %collective-permute-start.8 = (bf16[4,256,256]{2,1,0:T(8,128)(2,1)S(1)}, bf16[4,256,256]{2,1,0:T(8,128)(2,1)S(1)}, u32[]{:S(2)}, u32[]{:S(2)}) collective-permute-start(bf16[4,256,256]{2,1,0:T(8,128)(2,1)S(1)} %get-tuple-element.48), channel_id=1, source_target_pairs={{0,64},{64,128},{128,192},{192,0},{1,65},{65,129},{129,193},{193,1... | collective-permute-start | bytes 1572872 | tf_op jit(solution)/shard_map/ppermute | solution.py:33
  38.2 13.5 %collective-permute-start.9 = (bf16[4,256,256]{2,1,0:T(8,128)(2,1)S(1)}, bf16[4,256,256]{2,1,0:T(8,128)(2,1)S(1)}, u32[]{:S(2)}, u32[]{:S(2)}) collective-permute-start(bf16[4,256,256]{2,1,0:T(8,128)(2,1)S(1)} %get-tuple-element.49), channel_id=1, source_target_pairs={{0,192},{64,0},{128,64},{192,128},{1,193},{65,1},{129,65},{193,129... | collective-permute-start | bytes 1572872 | tf_op jit(solution)/shard_map/ppermute | solution.py:33
  48.9 12.7 %collective-permute-start.4 = (bf16[4,256,256]{2,1,0:T(8,128)(2,1)S(1)}, bf16[4,256,256]{2,1,0:T(8,128)(2,1)S(1)}, u32[]{:S(2)}, u32[]{:S(2)}) collective-permute-start(bf16[4,256,256]{2,1,0:T(8,128)(2,1)S(1)} %get-tuple-element.40), channel_id=1, source_target_pairs={{0,64},{64,128},{128,192},{192,0},{1,65},{65,129},{129,193},{193,1... | collective-permute-start | bytes 1572872 | tf_op jit(solution)/shard_map/ppermute | solution.py:33
  50.2 11.4 %collective-permute-start.5 = (bf16[4,256,256]{2,1,0:T(8,128)(2,1)S(1)}, bf16[4,256,256]{2,1,0:T(8,128)(2,1)S(1)}, u32[]{:S(2)}, u32[]{:S(2)}) collective-permute-start(bf16[4,256,256]{2,1,0:T(8,128)(2,1)S(1)} %get-tuple-element.41), channel_id=1, source_target_pairs={{0,192},{64,0},{128,64},{192,128},{1,193},{65,1},{129,65},{193,129... | collective-permute-start | bytes 1572872 | tf_op jit(solution)/shard_map/ppermute | solution.py:33
  51.8 15.4 %collective-permute-start.12 = (bf16[2,256,256]{2,1,0:T(8,128)(2,1)S(1)}, bf16[2,256,256]{2,1,0:T(8,128)(2,1)S(1)}, u32[]{:S(2)}, u32[]{:S(2)}) collective-permute-start(bf16[2,256,256]{2,1,0:T(8,128)(2,1)S(1)} %get-tuple-element.58), channel_id=1, source_target_pairs={{0,64},{64,128},{128,192},{192,0},{1,65},{65,129},{129,193},{193,1... | collective-permute-start | bytes 786440 | tf_op jit(solution)/shard_map/ppermute | solution.py:33
  61.8 11.3 %collective-permute-start.6 = (bf16[2,256,256]{2,1,0:T(8,128)(2,1)S(1)}, bf16[2,256,256]{2,1,0:T(8,128)(2,1)S(1)}, u32[]{:S(2)}, u32[]{:S(2)}) collective-permute-start(bf16[2,256,256]{2,1,0:T(8,128)(2,1)S(1)} %get-tuple-element.46), channel_id=1, source_target_pairs={{0,64},{64,128},{128,192},{192,0},{1,65},{65,129},{129,193},{193,1... | collective-permute-start | bytes 786440 | tf_op jit(solution)/shard_map/ppermute | solution.py:33
  63.2 15.5 %collective-permute-start.11 = (bf16[2,256,256]{2,1,0:T(8,128)(2,1)S(1)}, bf16[2,256,256]{2,1,0:T(8,128)(2,1)S(1)}, u32[]{:S(2)}, u32[]{:S(2)}) collective-permute-start(bf16[2,256,256]{2,1,0:T(8,128)(2,1)S(1)} %get-tuple-element.56), channel_id=1, source_target_pairs={{0,192},{64,0},{128,64},{192,128},{1,193},{65,1},{129,65},{193,129... | collective-permute-start | bytes 786440 | tf_op jit(solution)/shard_map/ppermute | solution.py:33
  64.5 14.1 %collective-permute-start.10 = (bf16[2,256,256]{2,1,0:T(8,128)(2,1)S(1)}, bf16[2,256,256]{2,1,0:T(8,128)(2,1)S(1)}, u32[]{:S(2)}, u32[]{:S(2)}) collective-permute-start(bf16[2,256,256]{2,1,0:T(8,128)(2,1)S(1)} %get-tuple-element.54), channel_id=1, source_target_pairs={{0,192},{64,0},{128,64},{192,128},{1,193},{65,1},{129,65},{193,129... | collective-permute-start | bytes 786440 | tf_op jit(solution)/shard_map/ppermute | solution.py:33
  67.4 11.8 %collective-permute-start.13 = (bf16[2,256,256]{2,1,0:T(8,128)(2,1)S(1)}, bf16[2,256,256]{2,1,0:T(8,128)(2,1)S(1)}, u32[]{:S(2)}, u32[]{:S(2)}) collective-permute-start(bf16[2,256,256]{2,1,0:T(8,128)(2,1)S(1)} %add_convert_fusion), channel_id=1, source_target_pairs={{0,63},{1,0},{2,1},{3,2},{4,3},{5,4},{6,5},{7,6},{8,7},{9,8},{10,9... | collective-permute-start | bytes 786440 | tf_op jit(solution)/shard_map/ppermute | solution.py:33
  73.2 11.6 %collective-permute-start.7 = (bf16[2,256,256]{2,1,0:T(8,128)(2,1)S(1)}, bf16[2,256,256]{2,1,0:T(8,128)(2,1)S(1)}, u32[]{:S(2)}, u32[]{:S(2)}) collective-permute-start(bf16[2,256,256]{2,1,0:T(8,128)(2,1)S(1)} %add_convert_fusion.1), channel_id=1, source_target_pairs={{0,63},{1,0},{2,1},{3,2},{4,3},{5,4},{6,5},{7,6},{8,7},{9,8},{10,9... | collective-permute-start | bytes 786440 | tf_op jit(solution)/shard_map/ppermute | solution.py:33

commit v3 on v2

--- a/solution.py
+++ b/solution.py
@@ -249,29 +249,39 @@
     )(cols_t, outcols_t, in_hbm(vals))
 
 
-TARGETS = {(2, 0): (0, 0), (1, 1): (0, 2), (2, 1): (1, 0), (3, 0): (1, 2)}
-TARGETS |= {(1, 0): (2, 0), (3, 1): (3, 0), (0, 0): (4, 0), (0, 1): (5, 0)}
-SIZES = (4, 4, 2, 2, 2, 2)
-
-
-def product_kernel(chunk, table, pool_in, listing, b_part, *rest):
-    a_parts, rest = rest[: chunk - 1], rest[chunk - 1 :]
-    outs, (pool, lines, away, right, twice, sem) = rest[:6], rest[6:]
+CALLS = {
+    "first": (1, {(2, 0): (0, 0), (1, 1): (0, 2), (2, 1): (1, 0), (3, 0): (1, 2)}, (4, 4)),
+    "rest": (1, {(1, 0): (0, 0), (3, 1): (1, 0), (0, 0): (2, 0), (0, 1): (3, 0)}, (2,) * 4),
+    "second": (
+        2,
+        {
+            **{(2, 0): (0, 0), (1, 1): (1, 0), (2, 1): (2, 0), (3, 0): (3, 0)},
+            **{(1, 0): (4, 0), (3, 1): (5, 0), (0, 0): (6, 0), (0, 1): (7, 0)},
+        },
+        (2,) * 8,
+    ),
+}
+
+
+def product_kernel(call, table, pool_in, listing, *rest):
+    chunk, targets, sizes = CALLS[call]
+    n_halo = {"first": 1, "rest": 0, "second": 2}[call]
+    halo, rest = rest[:n_halo], rest[n_halo:]
+    outs, (pool, lines, away, right, twice, sem) = rest[: len(sizes)], rest[len(sizes) :]
     layer, _ = here()
     first_rows = A_PARTS[0] * B
     listed = pltpu.make_async_copy(listing.at[pl.ds(first_rows, 16)], lines, sem.at[0])
     listed.start()
-    start = B0 + sum(B_PARTS[: chunk - 1])
-    pieces = [(b_part, start, B_PARTS[chunk - 1])]
-    if chunk == 1:
-        pieces += [(listing.at[pl.ds(p * B, B)], A0 + p, 0) for p in range(A_PARTS[0])]
-    else:
-        pieces += [(a_parts[0], A0 + A_PARTS[0], A_PARTS[1])]
+    pieces = []
+    if call == "first":
+        pieces = [(halo[0], pool.at[B0 : B0 + B_PARTS[0]])]
+        pieces += [(listing.at[pl.ds(p * B, B)], pool.at[A0 + p]) for p in range(A_PARTS[0])]
+    elif call == "second":
+        a_at, b_at = A0 + A_PARTS[0], B0 + B_PARTS[0]
+        pieces = [(halo[0], pool.at[b_at : b_at + B_PARTS[1]])]
+        pieces += [(halo[1], pool.at[a_at : a_at + A_PARTS[1]])]
     copies = [
-        pltpu.make_async_copy(
-            ref, pool.at[start : start + size] if size else pool.at[start], sem.at[1 + x]
-        )
-        for x, (ref, start, size) in enumerate(pieces)
+        pltpu.make_async_copy(ref, dst, sem.at[1 + x]) for x, (ref, dst) in enumerate(pieces)
     ]
     for copy in copies:
         copy.start()
@@ -290,9 +300,10 @@
         def store(at, value):
             twice[at] = value
 
-        for o in range(4):
-            far = away[(i + 4) * 4 + o, 0]
-            row_entries(i, far, layer, table, left, right, store, r * 4 + o)
+        for shift, above in targets:
+            if not above:
+                far = away[(i + 4) * 4 + ((layer + shift) & 3), 0]
+                row_entries(i, far, layer, table, left, right, store, r * 4 + shift)
         return carry
 
     lax.fori_loop(0, 2, below_row, 0)
@@ -303,19 +314,22 @@
         i = row_of(above, r)
         lefts = [table[LEFT + (i + 4) * 4 + t] for t in range(4)]
         for shift in (2, 1, 3, 0):
+            if (shift, above) not in targets:
+                continue
             o = (layer + shift) & 3
             acc = jnp.zeros((B, B), F32)
             for t in range(4):
-                place = table[(i * 4 + o) * 4 + t] if above else right[(r * 4 + o) * 4 + t]
+                at = (i * 4 + o) * 4 + t if above else (r * 4 + shift) * 4 + t
+                place = table[at] if above else right[at]
                 acc += lax.dot_general(
                     pool[lefts[t]],
                     pool[place],
                     (((1,), (1,)), ((), ())),
                     preferred_element_type=F32,
                 )
-            own = table[TWICE + i * 4 + o] if above else twice[r * 4 + o]
+            own = table[TWICE + i * 4 + o] if above else twice[r * 4 + shift]
             factor = jnp.where(own < ZERO, 2.0, 0.0).astype(F32)
-            out, start = TARGETS[shift, above]
+            out, start = targets[shift, above]
             outs[out][start + r] = (factor * pool[own].astype(F32) - acc).astype(BF)
         return carry
 
@@ -323,12 +337,13 @@
     lax.fori_loop(0, 2, functools.partial(compute, 1), 0)
 
 
-def products(table, pool, halo, chunk, name):
-    return pl.pallas_call(
-        functools.partial(product_kernel, chunk),
-        out_shape=[jax.ShapeDtypeStruct((n, B, B), BF) for n in (*SIZES, POOL)],
+def products(table, pool, halo, call):
+    sizes = CALLS[call][2]
+    return pl.pallas_call(
+        functools.partial(product_kernel, call),
+        out_shape=[jax.ShapeDtypeStruct((n, B, B), BF) for n in (*sizes, POOL)],
         in_specs=[SM, VM] + [ANY] * len(halo),
-        out_specs=[VM] * (len(SIZES) + 1),
+        out_specs=[VM] * (len(sizes) + 1),
         scratch_shapes=[
             pltpu.VMEM((16, B), BF),
             pltpu.VMEM((16, 128), I32),
@@ -336,15 +351,32 @@
             pltpu.SMEM((8,), I32),
             pltpu.SemaphoreType.DMA((2 + A_PARTS[0],)),
         ],
-        input_output_aliases={1: len(SIZES)},
+        input_output_aliases={1: len(sizes)},
+        compiler_params=pltpu.CompilerParams(vmem_limit_bytes=4 << 20),
+        cost_estimate=NOTHING,
+        name=f"products_{call}",
+    )(table, pool, *halo)
+
+
+def total(*parts):
+    return sum(part.astype(F32) for part in parts).astype(BF)
+
+
+def add_kernel(*refs):
+    parts, out = refs[:-1], refs[-1]
+    out[...] = total(*[part[...] for part in parts])
+
+
+def add(parts, name):
+    return pl.pallas_call(
+        add_kernel,
+        out_shape=jax.ShapeDtypeStruct((2, B, B), BF),
+        in_specs=[VM] * len(parts),
+        out_specs=VM,
         compiler_params=pltpu.CompilerParams(vmem_limit_bytes=4 << 20),
         cost_estimate=NOTHING,
         name=name,
-    )(table, pool, *halo)
-
-
-def total(*parts):
-    return sum(part.astype(F32) for part in parts).astype(BF)
+    )(*parts)
 
 
 def adds_kernel(a, b, c, d, x, y):
@@ -380,7 +412,7 @@
     for x, rows in enumerate(sums):
         own, plus, minus = parts[3 * x : 3 * x + 3]
         for r in range(2):
-            block[2 * x + r] = total(own[r], plus[2 + r], minus[r])
+            block[2 * x + r] = total(own[r], plus[plus.shape[0] - 2 + r], minus[r])
             send(block.at[2 * x + r], rows[r])
     for copy in copies:
         copy.wait()
@@ -413,27 +445,25 @@
     b2 = shifted(b2, ROWS, -1, False)
     table, pool = prepare(cols.T, outcols.T, vals)
 
-    out1 = products(table, pool, (a1, b1), 1, "products1")
-    plus1, minus1, up_b1, down1, own_b1, own1, pool = out1
+    plus1, minus1, pool = products(table, pool, (a1, b1), "first")
     plus1, minus1 = shifted(plus1, "layer", 1), shifted(minus1, "layer", -1)
-    out2 = products(table, pool, (a1, b2, a2), 2, "products2")
-    plus2, minus2, up_b2, down2, own_b2, own2, pool = out2
+    up_b1, down1, own_b1, own1, pool = products(table, pool, (a1,), "rest")
+    out2 = products(table, pool, (a1, b2, a2), "second")
+    far_b2, up2, far2, down_b2, up_b2, down2, own_b2, own2, pool = out2
     (plus1, minus1), _ = both(((plus1, minus1), own_b2))
-    plus2, minus2 = shifted(plus2, "layer", 1), shifted(minus2, "layer", -1)
-
-    def second(plus, minus, up_below, down, own_below, name, cost):
-        up_below, down = adds(up_below, plus, down, minus, name, cost)
-        up_below = shifted(up_below, "layer", 1)
-        down = shifted(down, "layer", -1)
-        below = shifted(total(own_below, minus[2:], up_below), ROWS, -1)
-        return down, below
-
-    down1, below1 = second(plus1, minus1, up_b1, down1, own_b1, "adds1", 40 << 20)
-    plus2, minus2 = both((plus2, minus2))
-    down2, below2 = second(plus2, minus2, up_b2, down2, own_b2, "adds2", 0)
-    parts = (own1, plus1, down1, own2, plus2, down2, below1)
-    mine = finish(((0, 1), (2, 3)), ((7, 6),), parts, (), "finish1")
-    mine = finish((), ((5, 4),), (below2,), (mine,), "finish2")
+    far_b2 = shifted(far_b2, "layer", 1)
+    down_b2 = shifted(down_b2, "layer", -1)
+    far2 = shifted(far2, "layer", -1)
+    up_b1, down1 = adds(up_b1, plus1, down1, minus1, "adds1", 40 << 20)
+    up_b1 = shifted(up_b1, "layer", 1)
+    down1 = shifted(down1, "layer", -1)
+    up_b2 = shifted(add((up_b2, far_b2), "add_below2"), "layer", 1)
+    up2 = shifted(up2, "layer", 1)
+    down2 = shifted(add((down2, far2), "add2"), "layer", -1)
+    below1 = shifted(total(own_b1, minus1[2:], up_b1), ROWS, -1)
+    below2 = shifted(add((own_b2, down_b2, up_b2), "below2"), ROWS, -1)
+    mine = finish(((0, 1),), ((7, 6),), (own1, plus1, down1, below1), (), "finish1")
+    mine = finish(((2, 3),), ((5, 4),), (own2, up2, down2, below2), (mine,), "finish2")
     return mine[:, None]
 
 

time: 86.1 us -> 79.6 us (0.925)
  waiting for transfers between devices: 30.7 us -> 21.4 us
  Pallas kernels: 18.2 us -> 19.8 us
    ppermute x14 -> x16, waiting for transfers between devices: 30.7 us -> 21.4 us  [shifted(): return lax.ppermute(value, axis, pairs)]
    pallas_call x2 -> x6, Pallas kernels: 9.97 us -> 11.7 us  [the longest x3 11.5 us: products(): pl.pallas_call(functools.partial(product_kernel, call), out_shape=[jax.Sh...]
    ppermute x14 -> x16, starting transfers between devices: 34.9 us -> 35.7 us  [shifted(): return lax.ppermute(value, axis, pairs)]
  transfers between devices with their start and end apart: 14 -> 16, of which waited for: 7 -> 7; matrix products, arithmetic and copies ran while one was open for 0% -> 0% of each run, Pallas kernels for 17% -> 20%
where the time goes in v3:
time: 79.6 us; the launch traced here: 78.6 us
  starting transfers between devices  35.7 us (45%)
  waiting for transfers between devices  21.4 us (27%)
  Pallas kernels  19.8 us (25%)
  local copies, waits for them, and re-layouts  1.36 us (2%)
    ppermute x16, starting transfers between devices, shifted(): return lax.ppermute(value, axis, pairs)  35.7 us
    ppermute x16, waiting for transfers between devices, shifted(): return lax.ppermute(value, axis, pairs)  21.4 us
    pallas_call x3, Pallas kernels, products(): pl.pallas_call(functools.partial(product_kernel, call), out_shape=[jax.Sh...  11.5 us
    pallas_call x1, Pallas kernels, prepare(): pl.pallas_call(prepare_kernel, out_shape=[jax.ShapeDtypeStruct((ENTRIES,)...  3.43 us
    pallas_call x1, Pallas kernels, pack(): pl.pallas_call(pack_kernel, out_shape=[jax.ShapeDtypeStruct(shape, BF) fo...  2.91 us
    pallas_call x2, Pallas kernels, finish(): pl.pallas_call(functools.partial(finish_kernel, sums, copied), out_shape=...  1.64 us
  transfers between devices with their start and end apart: 16, of which 7 were waited for; matrix products, arithmetic and copies ran while one was open for 0% of the time, Pallas kernels for 20%

profile of v3, /device:TPU:1, one launch (start us, length us, event | category | flops | bytes accessed | tf_op | source)
XLA Modules:
  0.0 78.6 jit_solution(5621585628529454962)
XLA Ops:
  0.0 2.9 %pack.1 = (bf16[1808,256]{1,0:T(8,128)(2,1)S(1)}, bf16[7,256,256]{2,1,0:T(8,128)(2,1)S(1)}, bf16[5,256,256]{2,1,0:T(8,128)(2,1)S(1)}, bf16[4,256,256]{2,1,0:T(8,128)(2,1)S(1)}) custom-call(s32[4,8]{1,0:T(4,128)} %bitcast.5, s32[4,8]{1,0:T(4,128)} %bitcast.7, bf16[8,4,256,256]{3,2,1,0:T(8,128)(2,1)} %vals.3), custom_call_target="tpu_custom_call" | custom-call | tf_op jit(solution)/shard_map/pack/pallas_call | solution.py:143
  2.9 2.5 %collective-permute-start = (bf16[1808,256]{1,0:T(8,128)(2,1)S(1)}, bf16[1808,256]{1,0:T(8,128)(2,1)S(1)}, u32[]{:S(2)}, u32[]{:S(2)}) collective-permute-start(bf16[1808,256]{1,0:T(8,128)(2,1)S(1)} %get-tuple-element.33), channel_id=1, source_target_pairs={{0,1},{1,2},{2,3},{3,4},{4,5},{5,6},{6,7},{7,8},{8,9},{9,10},{10,1... | collective-permute-start | bytes 2777096 | tf_op jit(solution)/shard_map/ppermute | solution.py:33
  5.5 6.4 %collective-permute-start.1 = (bf16[7,256,256]{2,1,0:T(8,128)(2,1)S(1)}, bf16[7,256,256]{2,1,0:T(8,128)(2,1)S(1)}, u32[]{:S(2)}, u32[]{:S(2)}) collective-permute-start(bf16[7,256,256]{2,1,0:T(8,128)(2,1)S(1)} %get-tuple-element.34), channel_id=1, source_target_pairs={{1,0},{2,1},{3,2},{4,3},{5,4},{6,5},{7,6},{8,7},{9,8},{10,9},{11,1... | collective-permute-start | bytes 2752520 | tf_op jit(solution)/shard_map/ppermute | solution.py:33
  12.0 4.8 %collective-permute-start.2 = (bf16[4,256,256]{2,1,0:T(8,128)(2,1)S(1)}, bf16[4,256,256]{2,1,0:T(8,128)(2,1)S(1)}, u32[]{:S(2)}, u32[]{:S(2)}) collective-permute-start(bf16[4,256,256]{2,1,0:T(8,128)(2,1)S(1)} %get-tuple-element.37), channel_id=1, source_target_pairs={{1,0},{2,1},{3,2},{4,3},{5,4},{6,5},{7,6},{8,7},{9,8},{10,9},{11,1... | collective-permute-start | bytes 1572872 | tf_op jit(solution)/shard_map/ppermute | solution.py:33
  18.2 3.4 %prepare.1 = (s32[144]{0:T(256)S(1)}, bf16[58,256,256]{2,1,0:T(8,128)(2,1)S(1)}) custom-call(s32[4,8]{1,0:T(4,128)S(1)} %bitcast.6, s32[4,8]{1,0:T(4,128)S(1)} %bitcast.8, bf16[8,4,256,256]{3,2,1,0:T(8,128)(2,1)} %vals.3), custom_call_target="tpu_custom_call" | custom-call | tf_op jit(solution)/shard_map/prepare/pallas_call | solution.py:237
  21.7 7.0 %collective-permute-done.1.rest_0_ = bf16[7,256,256]{2,1,0:T(8,128)(2,1)S(1)} collective-permute-done((bf16[7,256,256]{2,1,0:T(8,128)(2,1)S(1)}, bf16[7,256,256]{2,1,0:T(8,128)(2,1)S(1)}, u32[]{:S(2)}, u32[]{:S(2)}) %collective-permute-start.1) | collective-permute-done | bytes 917536 | tf_op jit(solution)/shard_map/ppermute | solution.py:33
  28.6 2.7 %collective-permute-done.listing = bf16[1808,256]{1,0:T(8,128)(2,1)S(1)} collective-permute-done((bf16[1808,256]{1,0:T(8,128)(2,1)S(1)}, bf16[1808,256]{1,0:T(8,128)(2,1)S(1)}, u32[]{:S(2)}, u32[]{:S(2)}) %collective-permute-start) | collective-permute-done | bytes 925728 | tf_op jit(solution)/shard_map/ppermute | solution.py:33
  31.3 4.3 %products_first.1 = (bf16[4,256,256]{2,1,0:T(8,128)(2,1)S(1)}, bf16[4,256,256]{2,1,0:T(8,128)(2,1)S(1)}, bf16[58,256,256]{2,1,0:T(8,128)(2,1)S(1)}) custom-call(s32[144]{0:T(256)S(1)} %get-tuple-element.31.table, bf16[58,256,256]{2,1,0:T(8,128)(2,1)S(1)} %get-tuple-element.32.pool_in, ...), custom_call_target="tpu_custom_call", output_to_operand_aliasing={{2}: (1, {})} | custom-call | tf_op jit(solution)/shard_map/products_first/pallas_call | solution.py:342
  35.6 1.3 %collective-permute-start.11 = (bf16[4,256,256]{2,1,0:T(8,128)(2,1)S(1)}, bf16[4,256,256]{2,1,0:T(8,128)(2,1)S(1)}, u32[]{:S(2)}, u32[]{:S(2)}) collective-permute-start(bf16[4,256,256]{2,1,0:T(8,128)(2,1)S(1)} %get-tuple-element.48), channel_id=1, source_target_pairs={{0,64},{64,128},{128,192},{192,0},{1,65},{65,129},{129,193},{193,1... | collective-permute-start | bytes 1572872 | tf_op jit(solution)/shard_map/ppermute | solution.py:33
  36.9 1.5 %collective-permute-start.12 = (bf16[4,256,256]{2,1,0:T(8,128)(2,1)S(1)}, bf16[4,256,256]{2,1,0:T(8,128)(2,1)S(1)}, u32[]{:S(2)}, u32[]{:S(2)}) collective-permute-start(bf16[4,256,256]{2,1,0:T(8,128)(2,1)S(1)} %get-tuple-element.49), channel_id=1, source_target_pairs={{0,192},{64,0},{128,64},{192,128},{1,193},{65,1},{129,65},{193,129... | collective-permute-start | bytes 1572872 | tf_op jit(solution)/shard_map/ppermute | solution.py:33
  38.3 2.8 %products_rest.1 = (bf16[2,256,256]{2,1,0:T(8,128)(2,1)S(1)}, bf16[2,256,256]{2,1,0:T(8,128)(2,1)S(1)}, bf16[2,256,256]{2,1,0:T(8,128)(2,1)S(1)}, bf16[2,256,256...) custom-call(s32[144]{0:T(256)S(1)} %get-tuple-element.31.table, ...), custom_call_target="tpu_custom_call", output_to_operand_aliasing={{4}: (1, {})} | custom-call | tf_op jit(solution)/shard_map/products_rest/pallas_call | solution.py:342
  41.2 3.3 %collective-permute-done.3.rest_1_ = bf16[5,256,256]{2,1,0:T(8,128)(2,1)S(1)} collective-permute-done((bf16[5,256,256]{2,1,0:T(8,128)(2,1)S(1)}, bf16[5,256,256]{2,1,0:T(8,128)(2,1)S(1)}, u32[]{:S(2)}, u32[]{:S(2)}) %collective-permute-start.3) | collective-permute-done | bytes 655392 | tf_op jit(solution)/shard_map/ppermute | solution.py:33
  44.5 4.4 %products_second.1 = (bf16[2,256,256]{2,1,0:T(8,128)(2,1)S(1)}, bf16[2,256,256]{2,1,0:T(8,128)(2,1)S(1)}, bf16[2,256,256]{2,1,0:T(8,128)(2,1)S(1)}, bf16[2,256,2...) custom-call(s32[144]{0:T(256)S(1)} %get-tuple-element.31.table, ...), custom_call_target="tpu_custom_call", output_to_operand_aliasing={{8}: (1, {})} | custom-call | tf_op jit(solution)/shard_map/products_second/pallas_call | solution.py:342
  48.9 1.3 %collective-permute-start.8 = (bf16[2,256,256]{2,1,0:T(8,128)(2,1)S(1)}, bf16[2,256,256]{2,1,0:T(8,128)(2,1)S(1)}, u32[]{:S(2)}, u32[]{:S(2)}) collective-permute-start(bf16[2,256,256]{2,1,0:T(8,128)(2,1)S(1)} %get-tuple-element.46), channel_id=1, source_target_pairs={{0,64},{64,128},{128,192},{192,0},{1,65},{65,129},{129,193},{193,1... | collective-permute-start | bytes 786440 | tf_op jit(solution)/shard_map/ppermute | solution.py:33
  50.2 1.5 %collective-permute-start.5 = (bf16[2,256,256]{2,1,0:T(8,128)(2,1)S(1)}, bf16[2,256,256]{2,1,0:T(8,128)(2,1)S(1)}, u32[]{:S(2)}, u32[]{:S(2)}) collective-permute-start(bf16[2,256,256]{2,1,0:T(8,128)(2,1)S(1)} %get-tuple-element.42), channel_id=1, source_target_pairs={{0,192},{64,0},{128,64},{192,128},{1,193},{65,1},{129,65},{193,129... | collective-permute-start | bytes 786440 | tf_op jit(solution)/shard_map/ppermute | solution.py:33
  51.9 2.6 %collective-permute-start.7 = (bf16[2,256,256]{2,1,0:T(8,128)(2,1)S(1)}, bf16[2,256,256]{2,1,0:T(8,128)(2,1)S(1)}, u32[]{:S(2)}, u32[]{:S(2)}) collective-permute-start(bf16[2,256,256]{2,1,0:T(8,128)(2,1)S(1)} %get-tuple-element.44), channel_id=1, source_target_pairs={{0,192},{64,0},{128,64},{192,128},{1,193},{65,1},{129,65},{193,129... | collective-permute-start | bytes 786440 | tf_op jit(solution)/shard_map/ppermute | solution.py:33
  54.6 1.4 %collective-permute-done.8.refs_1_ = bf16[2,256,256]{2,1,0:T(8,128)(2,1)S(1)} collective-permute-done((bf16[2,256,256]{2,1,0:T(8,128)(2,1)S(1)}, bf16[2,256,256]{2,1,0:T(8,128)(2,1)S(1)}, u32[]{:S(2)}, u32[]{:S(2)}) %collective-permute-start.8) | collective-permute-done | bytes 262176 | tf_op jit(solution)/shard_map/ppermute | solution.py:33
  57.1 2.1 %collective-permute-start.13 = (bf16[2,256,256]{2,1,0:T(8,128)(2,1)S(1)}, bf16[2,256,256]{2,1,0:T(8,128)(2,1)S(1)}, u32[]{:S(2)}, u32[]{:S(2)}) collective-permute-start(bf16[2,256,256]{2,1,0:T(8,128)(2,1)S(1)} %get-tuple-element.54), channel_id=1, source_target_pairs={{0,192},{64,0},{128,64},{192,128},{1,193},{65,1},{129,65},{193,129... | collective-permute-start | bytes 786440 | tf_op jit(solution)/shard_map/ppermute | solution.py:33
  59.2 2.4 %collective-permute-done.14 = bf16[2,256,256]{2,1,0:T(8,128)(2,1)S(1)} collective-permute-done((bf16[2,256,256]{2,1,0:T(8,128)(2,1)S(1)}, bf16[2,256,256]{2,1,0:T(8,128)(2,1)S(1)}, u32[]{:S(2)}, u32[]{:S(2)}) %collective-permute-start.14) | collective-permute-done | bytes 262176 | tf_op jit(solution)/shard_map/ppermute | solution.py:33
  61.7 4.9 %collective-permute-start.15 = (bf16[2,256,256]{2,1,0:T(8,128)(2,1)S(1)}, bf16[2,256,256]{2,1,0:T(8,128)(2,1)S(1)}, u32[]{:S(2)}, u32[]{:S(2)}) collective-permute-start(bf16[2,256,256]{2,1,0:T(8,128)(2,1)S(1)} %add_convert_fusion), channel_id=1, source_target_pairs={{0,63},{1,0},{2,1},{3,2},{4,3},{5,4},{6,5},{7,6},{8,7},{9,8},{10,9... | collective-permute-start | bytes 786440 | tf_op jit(solution)/shard_map/ppermute | solution.py:33
  66.7 1.3 %collective-permute-start.6 = (bf16[2,256,256]{2,1,0:T(8,128)(2,1)S(1)}, bf16[2,256,256]{2,1,0:T(8,128)(2,1)S(1)}, u32[]{:S(2)}, u32[]{:S(2)}) collective-permute-start(bf16[2,256,256]{2,1,0:T(8,128)(2,1)S(1)} %add2.1), channel_id=1, source_target_pairs={{0,192},{64,0},{128,64},{192,128},{1,193},{65,1},{129,65},{193,129... | collective-permute-start | bytes 786440 | tf_op jit(solution)/shard_map/ppermute | solution.py:33
  68.1 4.2 %collective-permute-start.10 = (bf16[2,256,256]{2,1,0:T(8,128)(2,1)S(1)}, bf16[2,256,256]{2,1,0:T(8,128)(2,1)S(1)}, u32[]{:S(2)}, u32[]{:S(2)}) collective-permute-start(bf16[2,256,256]{2,1,0:T(8,128)(2,1)S(1)} %below2.1), channel_id=1, source_target_pairs={{0,63},{1,0},{2,1},{3,2},{4,3},{5,4},{6,5},{7,6},{8,7},{9,8},{10,9... | collective-permute-start | bytes 786440 | tf_op jit(solution)/shard_map/ppermute | solution.py:33
  73.1 1.9 %collective-permute-done.6.rest_2_ = bf16[2,256,256]{2,1,0:T(8,128)(2,1)S(1)} collective-permute-done((bf16[2,256,256]{2,1,0:T(8,128)(2,1)S(1)}, bf16[2,256,256]{2,1,0:T(8,128)(2,1)S(1)}, u32[]{:S(2)}, u32[]{:S(2)}) %collective-permute-start.6) | collective-permute-done | bytes 262176 | tf_op jit(solution)/shard_map/ppermute | solution.py:33
  75.1 2.6 %collective-permute-done.10.rest_3_ = bf16[2,256,256]{2,1,0:T(8,128)(2,1)S(1)} collective-permute-done((bf16[2,256,256]{2,1,0:T(8,128)(2,1)S(1)}, bf16[2,256,256]{2,1,0:T(8,128)(2,1)S(1)}, u32[]{:S(2)}, u32[]{:S(2)}) %collective-permute-start.10) | collective-permute-done | bytes 262176 | tf_op jit(solution)/shard_map/ppermute | solution.py:33
  (24 shorter events, 4.7 us)
Async XLA Ops:
  2.9 28.4 %collective-permute-start = (bf16[1808,256]{1,0:T(8,128)(2,1)S(1)}, bf16[1808,256]{1,0:T(8,128)(2,1)S(1)}, u32[]{:S(2)}, u32[]{:S(2)}) collective-permute-start(bf16[1808,256]{1,0:T(8,128)(2,1)S(1)} %get-tuple-element.33), channel_id=1, source_target_pairs={{0,1},{1,2},{2,3},{3,4},{4,5},{5,6},{6,7},{7,8},{8,9},{9,10},{10,1... | collective-permute-start | bytes 2777096 | tf_op jit(solution)/shard_map/ppermute | solution.py:33
  5.5 23.2 %collective-permute-start.1 = (bf16[7,256,256]{2,1,0:T(8,128)(2,1)S(1)}, bf16[7,256,256]{2,1,0:T(8,128)(2,1)S(1)}, u32[]{:S(2)}, u32[]{:S(2)}) collective-permute-start(bf16[7,256,256]{2,1,0:T(8,128)(2,1)S(1)} %get-tuple-element.34), channel_id=1, source_target_pairs={{1,0},{2,1},{3,2},{4,3},{5,4},{6,5},{7,6},{8,7},{9,8},{10,9},{11,1... | collective-permute-start | bytes 2752520 | tf_op jit(solution)/shard_map/ppermute | solution.py:33
  11.9 32.6 %collective-permute-start.3 = (bf16[5,256,256]{2,1,0:T(8,128)(2,1)S(1)}, bf16[5,256,256]{2,1,0:T(8,128)(2,1)S(1)}, u32[]{:S(2)}, u32[]{:S(2)}) collective-permute-start(bf16[5,256,256]{2,1,0:T(8,128)(2,1)S(1)} %get-tuple-element.38), channel_id=1, source_target_pairs={{0,1},{1,2},{2,3},{3,4},{4,5},{5,6},{6,7},{7,8},{8,9},{9,10},{10,1... | collective-permute-start | bytes 1966088 | tf_op jit(solution)/shard_map/ppermute | solution.py:33
  12.0 29.2 %collective-permute-start.2 = (bf16[4,256,256]{2,1,0:T(8,128)(2,1)S(1)}, bf16[4,256,256]{2,1,0:T(8,128)(2,1)S(1)}, u32[]{:S(2)}, u32[]{:S(2)}) collective-permute-start(bf16[4,256,256]{2,1,0:T(8,128)(2,1)S(1)} %get-tuple-element.37), channel_id=1, source_target_pairs={{1,0},{2,1},{3,2},{4,3},{5,4},{6,5},{7,6},{8,7},{9,8},{10,9},{11,1... | collective-permute-start | bytes 1572872 | tf_op jit(solution)/shard_map/ppermute | solution.py:33
  16.9 0.7 copy-start
  17.5 0.7 copy-start.1
  35.6 16.1 %collective-permute-start.11 = (bf16[4,256,256]{2,1,0:T(8,128)(2,1)S(1)}, bf16[4,256,256]{2,1,0:T(8,128)(2,1)S(1)}, u32[]{:S(2)}, u32[]{:S(2)}) collective-permute-start(bf16[4,256,256]{2,1,0:T(8,128)(2,1)S(1)} %get-tuple-element.48), channel_id=1, source_target_pairs={{0,64},{64,128},{128,192},{192,0},{1,65},{65,129},{129,193},{193,1... | collective-permute-start | bytes 1572872 | tf_op jit(solution)/shard_map/ppermute | solution.py:33
  36.9 14.8 %collective-permute-start.12 = (bf16[4,256,256]{2,1,0:T(8,128)(2,1)S(1)}, bf16[4,256,256]{2,1,0:T(8,128)(2,1)S(1)}, u32[]{:S(2)}, u32[]{:S(2)}) collective-permute-start(bf16[4,256,256]{2,1,0:T(8,128)(2,1)S(1)} %get-tuple-element.49), channel_id=1, source_target_pairs={{0,192},{64,0},{128,64},{192,128},{1,193},{65,1},{129,65},{193,129... | collective-permute-start | bytes 1572872 | tf_op jit(solution)/shard_map/ppermute | solution.py:33
  48.9 7.1 %collective-permute-start.8 = (bf16[2,256,256]{2,1,0:T(8,128)(2,1)S(1)}, bf16[2,256,256]{2,1,0:T(8,128)(2,1)S(1)}, u32[]{:S(2)}, u32[]{:S(2)}) collective-permute-start(bf16[2,256,256]{2,1,0:T(8,128)(2,1)S(1)} %get-tuple-element.46), channel_id=1, source_target_pairs={{0,64},{64,128},{128,192},{192,0},{1,65},{65,129},{129,193},{193,1... | collective-permute-start | bytes 786440 | tf_op jit(solution)/shard_map/ppermute | solution.py:33
  50.2 6.9 %collective-permute-start.5 = (bf16[2,256,256]{2,1,0:T(8,128)(2,1)S(1)}, bf16[2,256,256]{2,1,0:T(8,128)(2,1)S(1)}, u32[]{:S(2)}, u32[]{:S(2)}) collective-permute-start(bf16[2,256,256]{2,1,0:T(8,128)(2,1)S(1)} %get-tuple-element.42), channel_id=1, source_target_pairs={{0,192},{64,0},{128,64},{192,128},{1,193},{65,1},{129,65},{193,129... | collective-permute-start | bytes 786440 | tf_op jit(solution)/shard_map/ppermute | solution.py:33
  51.8 9.8 %collective-permute-start.14 = (bf16[2,256,256]{2,1,0:T(8,128)(2,1)S(1)}, bf16[2,256,256]{2,1,0:T(8,128)(2,1)S(1)}, u32[]{:S(2)}, u32[]{:S(2)}) collective-permute-start(bf16[2,256,256]{2,1,0:T(8,128)(2,1)S(1)} %get-tuple-element.56), channel_id=1, source_target_pairs={{0,64},{64,128},{128,192},{192,0},{1,65},{65,129},{129,193},{193,1... | collective-permute-start | bytes 786440 | tf_op jit(solution)/shard_map/ppermute | solution.py:33
  51.9 14.8 %collective-permute-start.7 = (bf16[2,256,256]{2,1,0:T(8,128)(2,1)S(1)}, bf16[2,256,256]{2,1,0:T(8,128)(2,1)S(1)}, u32[]{:S(2)}, u32[]{:S(2)}) collective-permute-start(bf16[2,256,256]{2,1,0:T(8,128)(2,1)S(1)} %get-tuple-element.44), channel_id=1, source_target_pairs={{0,192},{64,0},{128,64},{192,128},{1,193},{65,1},{129,65},{193,129... | collective-permute-start | bytes 786440 | tf_op jit(solution)/shard_map/ppermute | solution.py:33
  56.1 11.9 %collective-permute-start.9 = (bf16[2,256,256]{2,1,0:T(8,128)(2,1)S(1)}, bf16[2,256,256]{2,1,0:T(8,128)(2,1)S(1)}, u32[]{:S(2)}, u32[]{:S(2)}) collective-permute-start(bf16[2,256,256]{2,1,0:T(8,128)(2,1)S(1)} %add_below2.1), channel_id=1, source_target_pairs={{0,64},{64,128},{128,192},{192,0},{1,65},{65,129},{129,193},{193,1... | collective-permute-start | bytes 786440 | tf_op jit(solution)/shard_map/ppermute | solution.py:33
  56.2 17.0 %collective-permute-start.4 = (bf16[2,256,256]{2,1,0:T(8,128)(2,1)S(1)}, bf16[2,256,256]{2,1,0:T(8,128)(2,1)S(1)}, u32[]{:S(2)}, u32[]{:S(2)}) collective-permute-start(bf16[2,256,256]{2,1,0:T(8,128)(2,1)S(1)} %get-tuple-element.40), channel_id=1, source_target_pairs={{0,64},{64,128},{128,192},{192,0},{1,65},{65,129},{129,193},{193,1... | collective-permute-start | bytes 786440 | tf_op jit(solution)/shard_map/ppermute | solution.py:33
  57.1 15.2 %collective-permute-start.13 = (bf16[2,256,256]{2,1,0:T(8,128)(2,1)S(1)}, bf16[2,256,256]{2,1,0:T(8,128)(2,1)S(1)}, u32[]{:S(2)}, u32[]{:S(2)}) collective-permute-start(bf16[2,256,256]{2,1,0:T(8,128)(2,1)S(1)} %get-tuple-element.54), channel_id=1, source_target_pairs={{0,192},{64,0},{128,64},{192,128},{1,193},{65,1},{129,65},{193,129... | collective-permute-start | bytes 786440 | tf_op jit(solution)/shard_map/ppermute | solution.py:33
  61.7 10.6 %collective-permute-start.15 = (bf16[2,256,256]{2,1,0:T(8,128)(2,1)S(1)}, bf16[2,256,256]{2,1,0:T(8,128)(2,1)S(1)}, u32[]{:S(2)}, u32[]{:S(2)}) collective-permute-start(bf16[2,256,256]{2,1,0:T(8,128)(2,1)S(1)} %add_convert_fusion), channel_id=1, source_target_pairs={{0,63},{1,0},{2,1},{3,2},{4,3},{5,4},{6,5},{7,6},{8,7},{9,8},{10,9... | collective-permute-start | bytes 786440 | tf_op jit(solution)/shard_map/ppermute | solution.py:33
  66.7 8.4 %collective-permute-start.6 = (bf16[2,256,256]{2,1,0:T(8,128)(2,1)S(1)}, bf16[2,256,256]{2,1,0:T(8,128)(2,1)S(1)}, u32[]{:S(2)}, u32[]{:S(2)}) collective-permute-start(bf16[2,256,256]{2,1,0:T(8,128)(2,1)S(1)} %add2.1), channel_id=1, source_target_pairs={{0,192},{64,0},{128,64},{192,128},{1,193},{65,1},{129,65},{193,129... | collective-permute-start | bytes 786440 | tf_op jit(solution)/shard_map/ppermute | solution.py:33
  68.1 9.6 %collective-permute-start.10 = (bf16[2,256,256]{2,1,0:T(8,128)(2,1)S(1)}, bf16[2,256,256]{2,1,0:T(8,128)(2,1)S(1)}, u32[]{:S(2)}, u32[]{:S(2)}) collective-permute-start(bf16[2,256,256]{2,1,0:T(8,128)(2,1)S(1)} %below2.1), channel_id=1, source_target_pairs={{0,63},{1,0},{2,1},{3,2},{4,3},{5,4},{6,5},{7,6},{8,7},{9,8},{10,9... | collective-permute-start | bytes 786440 | tf_op jit(solution)/shard_map/ppermute | solution.py:33

commit v4 on v3

--- a/solution.py
+++ b/solution.py
@@ -252,20 +252,18 @@
 CALLS = {
     "first": (1, {(2, 0): (0, 0), (1, 1): (0, 2), (2, 1): (1, 0), (3, 0): (1, 2)}, (4, 4)),
     "rest": (1, {(1, 0): (0, 0), (3, 1): (1, 0), (0, 0): (2, 0), (0, 1): (3, 0)}, (2,) * 4),
-    "second": (
+    "second": (2, {(2, 0): (0, 0), (2, 1): (1, 0), (3, 0): (2, 0)}, (2,) * 3),
+    "last": (
         2,
-        {
-            **{(2, 0): (0, 0), (1, 1): (1, 0), (2, 1): (2, 0), (3, 0): (3, 0)},
-            **{(1, 0): (4, 0), (3, 1): (5, 0), (0, 0): (6, 0), (0, 1): (7, 0)},
-        },
-        (2,) * 8,
+        {(1, 0): (0, 0), (1, 1): (1, 0), (3, 1): (2, 0), (0, 0): (3, 0), (0, 1): (4, 0)},
+        (2,) * 5,
     ),
 }
 
 
 def product_kernel(call, table, pool_in, listing, *rest):
     chunk, targets, sizes = CALLS[call]
-    n_halo = {"first": 1, "rest": 0, "second": 2}[call]
+    n_halo = {"first": 1, "second": 2}.get(call, 0)
     halo, rest = rest[:n_halo], rest[n_halo:]
     outs, (pool, lines, away, right, twice, sem) = rest[: len(sizes)], rest[len(sizes) :]
     layer, _ = here()
@@ -275,7 +273,8 @@
     pieces = []
     if call == "first":
         pieces = [(halo[0], pool.at[B0 : B0 + B_PARTS[0]])]
-        pieces += [(listing.at[pl.ds(p * B, B)], pool.at[A0 + p]) for p in range(A_PARTS[0])]
+        flat = pool.reshape(POOL * B, B)
+        pieces += [(listing.at[pl.ds(0, first_rows)], flat.at[pl.ds(A0 * B, first_rows)])]
     elif call == "second":
         a_at, b_at = A0 + A_PARTS[0], B0 + B_PARTS[0]
         pieces = [(halo[0], pool.at[b_at : b_at + B_PARTS[1]])]
@@ -289,7 +288,7 @@
     away[...] = lines[:, :128].astype(F32).astype(I32)
 
     def row_of(above, r):
-        return r + 2 * (chunk - 1) if above else -1 - r - 2 * (chunk - 1)
+        return r + 2 * (chunk - 1) if above else r - 2 * chunk
 
     def below_row(r, carry):
         i = row_of(0, r)
@@ -307,8 +306,6 @@
         return carry
 
     lax.fori_loop(0, 2, below_row, 0)
-    for copy in copies:
-        copy.wait()
 
     def compute(above, r, carry):
         i = row_of(above, r)
@@ -333,8 +330,13 @@
             outs[out][start + r] = (factor * pool[own].astype(F32) - acc).astype(BF)
         return carry
 
+    n_b = min(n_halo, 1)
+    for copy in copies[:n_b]:
+        copy.wait()
+    lax.fori_loop(0, 2, functools.partial(compute, 1), 0)
+    for copy in copies[n_b:]:
+        copy.wait()
     lax.fori_loop(0, 2, functools.partial(compute, 0), 0)
-    lax.fori_loop(0, 2, functools.partial(compute, 1), 0)
 
 
 def products(table, pool, halo, call):
@@ -349,7 +351,7 @@
             pltpu.VMEM((16, 128), I32),
             pltpu.SMEM((32,), I32),
             pltpu.SMEM((8,), I32),
-            pltpu.SemaphoreType.DMA((2 + A_PARTS[0],)),
+            pltpu.SemaphoreType.DMA((3,)),
         ],
         input_output_aliases={1: len(sizes)},
         compiler_params=pltpu.CompilerParams(vmem_limit_bytes=4 << 20),
@@ -396,39 +398,24 @@
     )(a, b, c, d)
 
 
-def finish_kernel(sums, copied, *rest):
-    n_in = 3 * len(sums) + len(copied)
-    parts, (out, block, sem) = rest[:n_in], rest[-3:]
-    copies = []
-
-    def send(src, row):
-        copy = pltpu.make_async_copy(src, out.at[row], sem.at[len(copies)])
-        copy.start()
-        copies.append(copy)
-
-    for x, rows in enumerate(copied):
-        for r in range(2):
-            send(parts[3 * len(sums) + x].at[r], rows[r])
-    for x, rows in enumerate(sums):
-        own, plus, minus = parts[3 * x : 3 * x + 3]
-        for r in range(2):
-            block[2 * x + r] = total(own[r], plus[plus.shape[0] - 2 + r], minus[r])
-            send(block.at[2 * x + r], rows[r])
-    for copy in copies:
-        copy.wait()
-
-
-def finish(sums, copied, parts, before, name):
-    n = 2 * len(sums) + 2 * len(copied)
-    return pl.pallas_call(
-        functools.partial(finish_kernel, sums, copied),
+def finish_kernel(row, below_row, own, plus, minus, below, *rest):
+    out, block, sem = rest[-3:]
+    whole = pltpu.make_async_copy(below, out.at[below_row : below_row + 2], sem.at[0])
+    whole.start()
+    block[...] = total(own[...], plus[plus.shape[0] - 2 :], minus[...])
+    summed = pltpu.make_async_copy(block, out.at[row : row + 2], sem.at[1])
+    summed.start()
+    whole.wait()
+    summed.wait()
+
+
+def finish(row, below_row, parts, before, name):
+    return pl.pallas_call(
+        functools.partial(finish_kernel, row, below_row),
         out_shape=jax.ShapeDtypeStruct((8, B, B), BF),
         in_specs=[VM] * len(parts) + [HBM] * len(before),
         out_specs=HBM,
-        scratch_shapes=[
-            pltpu.VMEM((max(2 * len(sums), 1), B, B), BF),
-            pltpu.SemaphoreType.DMA((n,)),
-        ],
+        scratch_shapes=[pltpu.VMEM((2, B, B), BF), pltpu.SemaphoreType.DMA((2,))],
         input_output_aliases={len(parts): 0} if before else {},
         compiler_params=pltpu.CompilerParams(vmem_limit_bytes=4 << 20),
         cost_estimate=NOTHING,
@@ -448,9 +435,9 @@
     plus1, minus1, pool = products(table, pool, (a1, b1), "first")
     plus1, minus1 = shifted(plus1, "layer", 1), shifted(minus1, "layer", -1)
     up_b1, down1, own_b1, own1, pool = products(table, pool, (a1,), "rest")
-    out2 = products(table, pool, (a1, b2, a2), "second")
-    far_b2, up2, far2, down_b2, up_b2, down2, own_b2, own2, pool = out2
-    (plus1, minus1), _ = both(((plus1, minus1), own_b2))
+    far_b2, far2, down_b2, pool = products(table, pool, (a1, b2, a2), "second")
+    up_b2, up2, down2, own_b2, own2, pool = products(table, pool, (a1,), "last")
+    (plus1, minus1), _ = both(((plus1, minus1), down_b2))
     far_b2 = shifted(far_b2, "layer", 1)
     down_b2 = shifted(down_b2, "layer", -1)
     far2 = shifted(far2, "layer", -1)
@@ -462,8 +449,8 @@
     down2 = shifted(add((down2, far2), "add2"), "layer", -1)
     below1 = shifted(total(own_b1, minus1[2:], up_b1), ROWS, -1)
     below2 = shifted(add((own_b2, down_b2, up_b2), "below2"), ROWS, -1)
-    mine = finish(((0, 1),), ((7, 6),), (own1, plus1, down1, below1), (), "finish1")
-    mine = finish(((2, 3),), ((5, 4),), (own2, up2, down2, below2), (mine,), "finish2")
+    mine = finish(0, 6, (own1, plus1, down1, below1), (), "finish1")
+    mine = finish(2, 4, (own2, up2, down2, below2), (mine,), "finish2")
     return mine[:, None]
 
 

time: 79.6 us -> 78.4 us (0.985)
  waiting for transfers between devices: 21.4 us -> 20.1 us
    ppermute x16, waiting for transfers between devices: 21.4 us -> 20.1 us  [shifted(): return lax.ppermute(value, axis, pairs)]
    pallas_call x3 -> x4, Pallas kernels: 11.5 us -> 11.8 us  [products(): pl.pallas_call(functools.partial(product_kernel, call), out_shape=[jax.Sh...]
  transfers between devices with their start and end apart: 16 -> 16, of which waited for: 7 -> 6; matrix products, arithmetic and copies ran while one was open for 0% -> 0% of each run, Pallas kernels for 20% -> 21%
where the time goes in v4:
time: 78.4 us; the launch traced here: 78.2 us
  starting transfers between devices  36.2 us (46%)
  Pallas kernels  20.2 us (26%)
  waiting for transfers between devices  20.1 us (26%)
  local copies, waits for them, and re-layouts  1.36 us (2%)
    ppermute x16, starting transfers between devices, shifted(): return lax.ppermute(value, axis, pairs)  36.2 us
    ppermute x16, waiting for transfers between devices, shifted(): return lax.ppermute(value, axis, pairs)  20.1 us
    pallas_call x4, Pallas kernels, products(): pl.pallas_call(functools.partial(product_kernel, call), out_shape=[jax.Sh...  11.8 us
    pallas_call x1, Pallas kernels, prepare(): pl.pallas_call(prepare_kernel, out_shape=[jax.ShapeDtypeStruct((ENTRIES,)...  3.43 us
    pallas_call x1, Pallas kernels, pack(): pl.pallas_call(pack_kernel, out_shape=[jax.ShapeDtypeStruct(shape, BF) fo...  2.91 us
    pallas_call x2, Pallas kernels, finish(): pl.pallas_call(functools.partial(finish_kernel, row, below_row), out_shap...  1.63 us
  transfers between devices with their start and end apart: 16, of which 6 were waited for; matrix products, arithmetic and copies ran while one was open for 0% of the time, Pallas kernels for 21%

profile of v4, /device:TPU:1, one launch (start us, length us, event | category | flops | bytes accessed | tf_op | source)
XLA Modules:
  0.0 78.2 jit_solution(12457916261959351246)
XLA Ops:
  0.0 2.9 %pack.1 = (bf16[1808,256]{1,0:T(8,128)(2,1)S(1)}, bf16[7,256,256]{2,1,0:T(8,128)(2,1)S(1)}, bf16[5,256,256]{2,1,0:T(8,128)(2,1)S(1)}, bf16[4,256,256]{2,1,0:T(8,128)(2,1)S(1)}) custom-call(s32[4,8]{1,0:T(4,128)} %bitcast.5, s32[4,8]{1,0:T(4,128)} %bitcast.7, bf16[8,4,256,256]{3,2,1,0:T(8,128)(2,1)} %vals.3), custom_call_target="tpu_custom_call" | custom-call | tf_op jit(solution)/shard_map/pack/pallas_call | solution.py:143
  2.9 2.5 %collective-permute-start = (bf16[1808,256]{1,0:T(8,128)(2,1)S(1)}, bf16[1808,256]{1,0:T(8,128)(2,1)S(1)}, u32[]{:S(2)}, u32[]{:S(2)}) collective-permute-start(bf16[1808,256]{1,0:T(8,128)(2,1)S(1)} %get-tuple-element.34), channel_id=1, source_target_pairs={{0,1},{1,2},{2,3},{3,4},{4,5},{5,6},{6,7},{7,8},{8,9},{9,10},{10,1... | collective-permute-start | bytes 2777096 | tf_op jit(solution)/shard_map/ppermute | solution.py:33
  5.5 6.4 %collective-permute-start.1 = (bf16[7,256,256]{2,1,0:T(8,128)(2,1)S(1)}, bf16[7,256,256]{2,1,0:T(8,128)(2,1)S(1)}, u32[]{:S(2)}, u32[]{:S(2)}) collective-permute-start(bf16[7,256,256]{2,1,0:T(8,128)(2,1)S(1)} %get-tuple-element.35), channel_id=1, source_target_pairs={{1,0},{2,1},{3,2},{4,3},{5,4},{6,5},{7,6},{8,7},{9,8},{10,9},{11,1... | collective-permute-start | bytes 2752520 | tf_op jit(solution)/shard_map/ppermute | solution.py:33
  12.0 4.8 %collective-permute-start.2 = (bf16[4,256,256]{2,1,0:T(8,128)(2,1)S(1)}, bf16[4,256,256]{2,1,0:T(8,128)(2,1)S(1)}, u32[]{:S(2)}, u32[]{:S(2)}) collective-permute-start(bf16[4,256,256]{2,1,0:T(8,128)(2,1)S(1)} %get-tuple-element.38), channel_id=1, source_target_pairs={{1,0},{2,1},{3,2},{4,3},{5,4},{6,5},{7,6},{8,7},{9,8},{10,9},{11,1... | collective-permute-start | bytes 1572872 | tf_op jit(solution)/shard_map/ppermute | solution.py:33
  18.2 3.4 %prepare.1 = (s32[144]{0:T(256)S(1)}, bf16[58,256,256]{2,1,0:T(8,128)(2,1)S(1)}) custom-call(s32[4,8]{1,0:T(4,128)S(1)} %bitcast.6, s32[4,8]{1,0:T(4,128)S(1)} %bitcast.8, bf16[8,4,256,256]{3,2,1,0:T(8,128)(2,1)} %vals.3), custom_call_target="tpu_custom_call" | custom-call | tf_op jit(solution)/shard_map/prepare/pallas_call | solution.py:237
  21.7 7.0 %collective-permute-done.1.rest_0_ = bf16[7,256,256]{2,1,0:T(8,128)(2,1)S(1)} collective-permute-done((bf16[7,256,256]{2,1,0:T(8,128)(2,1)S(1)}, bf16[7,256,256]{2,1,0:T(8,128)(2,1)S(1)}, u32[]{:S(2)}, u32[]{:S(2)}) %collective-permute-start.1) | collective-permute-done | bytes 917536 | tf_op jit(solution)/shard_map/ppermute | solution.py:33
  28.6 2.7 %collective-permute-done.listing = bf16[1808,256]{1,0:T(8,128)(2,1)S(1)} collective-permute-done((bf16[1808,256]{1,0:T(8,128)(2,1)S(1)}, bf16[1808,256]{1,0:T(8,128)(2,1)S(1)}, u32[]{:S(2)}, u32[]{:S(2)}) %collective-permute-start) | collective-permute-done | bytes 925728 | tf_op jit(solution)/shard_map/ppermute | solution.py:33
  31.3 3.2 %products_first.1 = (bf16[4,256,256]{2,1,0:T(8,128)(2,1)S(1)}, bf16[4,256,256]{2,1,0:T(8,128)(2,1)S(1)}, bf16[58,256,256]{2,1,0:T(8,128)(2,1)S(1)}) custom-call(s32[144]{0:T(256)S(1)} %get-tuple-element.32.table, bf16[58,256,256]{2,1,0:T(8,128)(2,1)S(1)} %get-tuple-element.33.pool_in, ...), custom_call_target="tpu_custom_call", output_to_operand_aliasing={{2}: (1, {})} | custom-call | tf_op jit(solution)/shard_map/products_first/pallas_call | solution.py:344
  34.6 1.3 %collective-permute-start.11 = (bf16[4,256,256]{2,1,0:T(8,128)(2,1)S(1)}, bf16[4,256,256]{2,1,0:T(8,128)(2,1)S(1)}, u32[]{:S(2)}, u32[]{:S(2)}) collective-permute-start(bf16[4,256,256]{2,1,0:T(8,128)(2,1)S(1)} %get-tuple-element.50), channel_id=1, source_target_pairs={{0,64},{64,128},{128,192},{192,0},{1,65},{65,129},{129,193},{193,1... | collective-permute-start | bytes 1572872 | tf_op jit(solution)/shard_map/ppermute | solution.py:33
  35.9 1.5 %collective-permute-start.12 = (bf16[4,256,256]{2,1,0:T(8,128)(2,1)S(1)}, bf16[4,256,256]{2,1,0:T(8,128)(2,1)S(1)}, u32[]{:S(2)}, u32[]{:S(2)}) collective-permute-start(bf16[4,256,256]{2,1,0:T(8,128)(2,1)S(1)} %get-tuple-element.51), channel_id=1, source_target_pairs={{0,192},{64,0},{128,64},{192,128},{1,193},{65,1},{129,65},{193,129... | collective-permute-start | bytes 1572872 | tf_op jit(solution)/shard_map/ppermute | solution.py:33
  37.3 2.8 %products_rest.1 = (bf16[2,256,256]{2,1,0:T(8,128)(2,1)S(1)}, bf16[2,256,256]{2,1,0:T(8,128)(2,1)S(1)}, bf16[2,256,256]{2,1,0:T(8,128)(2,1)S(1)}, bf16[2,256,256...) custom-call(s32[144]{0:T(256)S(1)} %get-tuple-element.32.table, ...), custom_call_target="tpu_custom_call", output_to_operand_aliasing={{4}: (1, {})} | custom-call | tf_op jit(solution)/shard_map/products_rest/pallas_call | solution.py:344
  40.1 4.4 %collective-permute-done.3.rest_1_ = bf16[5,256,256]{2,1,0:T(8,128)(2,1)S(1)} collective-permute-done((bf16[5,256,256]{2,1,0:T(8,128)(2,1)S(1)}, bf16[5,256,256]{2,1,0:T(8,128)(2,1)S(1)}, u32[]{:S(2)}, u32[]{:S(2)}) %collective-permute-start.3) | collective-permute-done | bytes 655392 | tf_op jit(solution)/shard_map/ppermute | solution.py:33
  44.5 2.8 %products_second.1 = (bf16[2,256,256]{2,1,0:T(8,128)(2,1)S(1)}, bf16[2,256,256]{2,1,0:T(8,128)(2,1)S(1)}, bf16[2,256,256]{2,1,0:T(8,128)(2,1)S(1)}, bf16[58,256,256]{2,1,0:T(8,128)(2,1)S(1)}) custom-call(s32[144]{0:T(256)S(1)} %get-tuple-element.32.table, bf16[58,256,256]{2,1,0:T(8,128)(2,1)S(1)} %get-tuple-element.37.pool_in, ...), custom_call_target="tpu_custom_call", output_to_operand_aliasing={{3}: (1, {})} | custom-call | tf_op jit(solution)/shard_map/products_second/pallas_call | solution.py:344
  47.3 1.3 %collective-permute-start.8 = (bf16[2,256,256]{2,1,0:T(8,128)(2,1)S(1)}, bf16[2,256,256]{2,1,0:T(8,128)(2,1)S(1)}, u32[]{:S(2)}, u32[]{:S(2)}) collective-permute-start(bf16[2,256,256]{2,1,0:T(8,128)(2,1)S(1)} %get-tuple-element.48), channel_id=1, source_target_pairs={{0,64},{64,128},{128,192},{192,0},{1,65},{65,129},{129,193},{193,1... | collective-permute-start | bytes 786440 | tf_op jit(solution)/shard_map/ppermute | solution.py:33
  48.6 1.5 %collective-permute-start.5 = (bf16[2,256,256]{2,1,0:T(8,128)(2,1)S(1)}, bf16[2,256,256]{2,1,0:T(8,128)(2,1)S(1)}, u32[]{:S(2)}, u32[]{:S(2)}) collective-permute-start(bf16[2,256,256]{2,1,0:T(8,128)(2,1)S(1)} %get-tuple-element.44), channel_id=1, source_target_pairs={{0,192},{64,0},{128,64},{192,128},{1,193},{65,1},{129,65},{193,129... | collective-permute-start | bytes 786440 | tf_op jit(solution)/shard_map/ppermute | solution.py:33
  50.3 2.6 %collective-permute-start.7 = (bf16[2,256,256]{2,1,0:T(8,128)(2,1)S(1)}, bf16[2,256,256]{2,1,0:T(8,128)(2,1)S(1)}, u32[]{:S(2)}, u32[]{:S(2)}) collective-permute-start(bf16[2,256,256]{2,1,0:T(8,128)(2,1)S(1)} %get-tuple-element.46), channel_id=1, source_target_pairs={{0,192},{64,0},{128,64},{192,128},{1,193},{65,1},{129,65},{193,129... | collective-permute-start | bytes 786440 | tf_op jit(solution)/shard_map/ppermute | solution.py:33
  53.0 3.1 %products_last.1 = (bf16[2,256,256]{2,1,0:T(8,128)(2,1)S(1)}, bf16[2,256,256]{2,1,0:T(8,128)(2,1)S(1)}, bf16[2,256,256]{2,1,0:T(8,128)(2,1)S(1)}, bf16[2,256,256...) custom-call(s32[144]{0:T(256)S(1)} %get-tuple-element.32.table, ...), custom_call_target="tpu_custom_call", output_to_operand_aliasing={{5}: (1, {})} | custom-call | tf_op jit(solution)/shard_map/products_last/pallas_call | solution.py:344
  56.5 2.7 %collective-permute-start.13 = (bf16[2,256,256]{2,1,0:T(8,128)(2,1)S(1)}, bf16[2,256,256]{2,1,0:T(8,128)(2,1)S(1)}, u32[]{:S(2)}, u32[]{:S(2)}) collective-permute-start(bf16[2,256,256]{2,1,0:T(8,128)(2,1)S(1)} %get-tuple-element.56), channel_id=1, source_target_pairs={{0,192},{64,0},{128,64},{192,128},{1,193},{65,1},{129,65},{193,129... | collective-permute-start | bytes 786440 | tf_op jit(solution)/shard_map/ppermute | solution.py:33
  60.2 5.0 %collective-permute-start.15 = (bf16[2,256,256]{2,1,0:T(8,128)(2,1)S(1)}, bf16[2,256,256]{2,1,0:T(8,128)(2,1)S(1)}, u32[]{:S(2)}, u32[]{:S(2)}) collective-permute-start(bf16[2,256,256]{2,1,0:T(8,128)(2,1)S(1)} %add_convert_fusion), channel_id=1, source_target_pairs={{0,63},{1,0},{2,1},{3,2},{4,3},{5,4},{6,5},{7,6},{8,7},{9,8},{10,9... | collective-permute-start | bytes 786440 | tf_op jit(solution)/shard_map/ppermute | solution.py:33
  65.2 1.2 %collective-permute-start.6 = (bf16[2,256,256]{2,1,0:T(8,128)(2,1)S(1)}, bf16[2,256,256]{2,1,0:T(8,128)(2,1)S(1)}, u32[]{:S(2)}, u32[]{:S(2)}) collective-permute-start(bf16[2,256,256]{2,1,0:T(8,128)(2,1)S(1)} %add2.1), channel_id=1, source_target_pairs={{0,192},{64,0},{128,64},{192,128},{1,193},{65,1},{129,65},{193,129... | collective-permute-start | bytes 786440 | tf_op jit(solution)/shard_map/ppermute | solution.py:33
  66.5 4.7 %collective-permute-start.10 = (bf16[2,256,256]{2,1,0:T(8,128)(2,1)S(1)}, bf16[2,256,256]{2,1,0:T(8,128)(2,1)S(1)}, u32[]{:S(2)}, u32[]{:S(2)}) collective-permute-start(bf16[2,256,256]{2,1,0:T(8,128)(2,1)S(1)} %below2.1), channel_id=1, source_target_pairs={{0,63},{1,0},{2,1},{3,2},{4,3},{5,4},{6,5},{7,6},{8,7},{9,8},{10,9... | collective-permute-start | bytes 786440 | tf_op jit(solution)/shard_map/ppermute | solution.py:33
  71.2 0.8 %finish1.1.rest_0_ = bf16[8,256,256]{2,1,0:T(8,128)(2,1)} custom-call(bf16[2,256,256]{2,1,0:T(8,128)(2,1)S(1)} %get-tuple-element.49.own, bf16[4,256,256]{2,1,0:T(8,128)(2,1)S(1)} %collective-permute-done.11.b.plus, bf16[2,256,256]{2,1,0:T(8,128)(2,1)S(1)} %collective-permute-done.13.minus, bf16[2,256,256]{2,1,0:T(8,128)(2,1)S(1)} %collective-permute-done.15.below), custom_call_target="tpu_custom_call" | custom-call | tf_op jit(solution)/shard_map/finish1/pallas_call | solution.py:413
  72.0 1.5 %collective-permute-done.6.minus = bf16[2,256,256]{2,1,0:T(8,128)(2,1)S(1)} collective-permute-done((bf16[2,256,256]{2,1,0:T(8,128)(2,1)S(1)}, bf16[2,256,256]{2,1,0:T(8,128)(2,1)S(1)}, u32[]{:S(2)}, u32[]{:S(2)}) %collective-permute-start.6) | collective-permute-done | bytes 262176 | tf_op jit(solution)/shard_map/ppermute | solution.py:33
  73.6 3.7 %collective-permute-done.10.below = bf16[2,256,256]{2,1,0:T(8,128)(2,1)S(1)} collective-permute-done((bf16[2,256,256]{2,1,0:T(8,128)(2,1)S(1)}, bf16[2,256,256]{2,1,0:T(8,128)(2,1)S(1)}, u32[]{:S(2)}, u32[]{:S(2)}) %collective-permute-start.10) | collective-permute-done | bytes 262176 | tf_op jit(solution)/shard_map/ppermute | solution.py:33
  (25 shorter events, 4.0 us)
Async XLA Ops:
  2.9 28.4 %collective-permute-start = (bf16[1808,256]{1,0:T(8,128)(2,1)S(1)}, bf16[1808,256]{1,0:T(8,128)(2,1)S(1)}, u32[]{:S(2)}, u32[]{:S(2)}) collective-permute-start(bf16[1808,256]{1,0:T(8,128)(2,1)S(1)} %get-tuple-element.34), channel_id=1, source_target_pairs={{0,1},{1,2},{2,3},{3,4},{4,5},{5,6},{6,7},{7,8},{8,9},{9,10},{10,1... | collective-permute-start | bytes 2777096 | tf_op jit(solution)/shard_map/ppermute | solution.py:33
  5.5 23.2 %collective-permute-start.1 = (bf16[7,256,256]{2,1,0:T(8,128)(2,1)S(1)}, bf16[7,256,256]{2,1,0:T(8,128)(2,1)S(1)}, u32[]{:S(2)}, u32[]{:S(2)}) collective-permute-start(bf16[7,256,256]{2,1,0:T(8,128)(2,1)S(1)} %get-tuple-element.35), channel_id=1, source_target_pairs={{1,0},{2,1},{3,2},{4,3},{5,4},{6,5},{7,6},{8,7},{9,8},{10,9},{11,1... | collective-permute-start | bytes 2752520 | tf_op jit(solution)/shard_map/ppermute | solution.py:33
  11.9 32.6 %collective-permute-start.3 = (bf16[5,256,256]{2,1,0:T(8,128)(2,1)S(1)}, bf16[5,256,256]{2,1,0:T(8,128)(2,1)S(1)}, u32[]{:S(2)}, u32[]{:S(2)}) collective-permute-start(bf16[5,256,256]{2,1,0:T(8,128)(2,1)S(1)} %get-tuple-element.39), channel_id=1, source_target_pairs={{0,1},{1,2},{2,3},{3,4},{4,5},{5,6},{6,7},{7,8},{8,9},{9,10},{10,1... | collective-permute-start | bytes 1966088 | tf_op jit(solution)/shard_map/ppermute | solution.py:33
  12.0 28.1 %collective-permute-start.2 = (bf16[4,256,256]{2,1,0:T(8,128)(2,1)S(1)}, bf16[4,256,256]{2,1,0:T(8,128)(2,1)S(1)}, u32[]{:S(2)}, u32[]{:S(2)}) collective-permute-start(bf16[4,256,256]{2,1,0:T(8,128)(2,1)S(1)} %get-tuple-element.38), channel_id=1, source_target_pairs={{1,0},{2,1},{3,2},{4,3},{5,4},{6,5},{7,6},{8,7},{9,8},{10,9},{11,1... | collective-permute-start | bytes 1572872 | tf_op jit(solution)/shard_map/ppermute | solution.py:33
  16.8 0.7 copy-start
  17.5 0.7 copy-start.1
  34.6 15.5 %collective-permute-start.11 = (bf16[4,256,256]{2,1,0:T(8,128)(2,1)S(1)}, bf16[4,256,256]{2,1,0:T(8,128)(2,1)S(1)}, u32[]{:S(2)}, u32[]{:S(2)}) collective-permute-start(bf16[4,256,256]{2,1,0:T(8,128)(2,1)S(1)} %get-tuple-element.50), channel_id=1, source_target_pairs={{0,64},{64,128},{128,192},{192,0},{1,65},{65,129},{129,193},{193,1... | collective-permute-start | bytes 1572872 | tf_op jit(solution)/shard_map/ppermute | solution.py:33
  35.9 14.2 %collective-permute-start.12 = (bf16[4,256,256]{2,1,0:T(8,128)(2,1)S(1)}, bf16[4,256,256]{2,1,0:T(8,128)(2,1)S(1)}, u32[]{:S(2)}, u32[]{:S(2)}) collective-permute-start(bf16[4,256,256]{2,1,0:T(8,128)(2,1)S(1)} %get-tuple-element.51), channel_id=1, source_target_pairs={{0,192},{64,0},{128,64},{192,128},{1,193},{65,1},{129,65},{193,129... | collective-permute-start | bytes 1572872 | tf_op jit(solution)/shard_map/ppermute | solution.py:33
  47.3 8.7 %collective-permute-start.8 = (bf16[2,256,256]{2,1,0:T(8,128)(2,1)S(1)}, bf16[2,256,256]{2,1,0:T(8,128)(2,1)S(1)}, u32[]{:S(2)}, u32[]{:S(2)}) collective-permute-start(bf16[2,256,256]{2,1,0:T(8,128)(2,1)S(1)} %get-tuple-element.48), channel_id=1, source_target_pairs={{0,64},{64,128},{128,192},{192,0},{1,65},{65,129},{129,193},{193,1... | collective-permute-start | bytes 786440 | tf_op jit(solution)/shard_map/ppermute | solution.py:33
  48.6 7.9 %collective-permute-start.5 = (bf16[2,256,256]{2,1,0:T(8,128)(2,1)S(1)}, bf16[2,256,256]{2,1,0:T(8,128)(2,1)S(1)}, u32[]{:S(2)}, u32[]{:S(2)}) collective-permute-start(bf16[2,256,256]{2,1,0:T(8,128)(2,1)S(1)} %get-tuple-element.44), channel_id=1, source_target_pairs={{0,192},{64,0},{128,64},{192,128},{1,193},{65,1},{129,65},{193,129... | collective-permute-start | bytes 786440 | tf_op jit(solution)/shard_map/ppermute | solution.py:33
  50.2 9.9 %collective-permute-start.14 = (bf16[2,256,256]{2,1,0:T(8,128)(2,1)S(1)}, bf16[2,256,256]{2,1,0:T(8,128)(2,1)S(1)}, u32[]{:S(2)}, u32[]{:S(2)}) collective-permute-start(bf16[2,256,256]{2,1,0:T(8,128)(2,1)S(1)} %get-tuple-element.58), channel_id=1, source_target_pairs={{0,64},{64,128},{128,192},{192,0},{1,65},{65,129},{129,193},{193,1... | collective-permute-start | bytes 786440 | tf_op jit(solution)/shard_map/ppermute | solution.py:33
  50.3 14.8 %collective-permute-start.7 = (bf16[2,256,256]{2,1,0:T(8,128)(2,1)S(1)}, bf16[2,256,256]{2,1,0:T(8,128)(2,1)S(1)}, u32[]{:S(2)}, u32[]{:S(2)}) collective-permute-start(bf16[2,256,256]{2,1,0:T(8,128)(2,1)S(1)} %get-tuple-element.46), channel_id=1, source_target_pairs={{0,192},{64,0},{128,64},{192,128},{1,193},{65,1},{129,65},{193,129... | collective-permute-start | bytes 786440 | tf_op jit(solution)/shard_map/ppermute | solution.py:33
  56.1 10.3 %collective-permute-start.9 = (bf16[2,256,256]{2,1,0:T(8,128)(2,1)S(1)}, bf16[2,256,256]{2,1,0:T(8,128)(2,1)S(1)}, u32[]{:S(2)}, u32[]{:S(2)}) collective-permute-start(bf16[2,256,256]{2,1,0:T(8,128)(2,1)S(1)} %add_below2.1), channel_id=1, source_target_pairs={{0,64},{64,128},{128,192},{192,0},{1,65},{65,129},{129,193},{193,1... | collective-permute-start | bytes 786440 | tf_op jit(solution)/shard_map/ppermute | solution.py:33
  56.2 15.8 %collective-permute-start.4 = (bf16[2,256,256]{2,1,0:T(8,128)(2,1)S(1)}, bf16[2,256,256]{2,1,0:T(8,128)(2,1)S(1)}, u32[]{:S(2)}, u32[]{:S(2)}) collective-permute-start(bf16[2,256,256]{2,1,0:T(8,128)(2,1)S(1)} %get-tuple-element.42), channel_id=1, source_target_pairs={{0,64},{64,128},{128,192},{192,0},{1,65},{65,129},{129,193},{193,1... | collective-permute-start | bytes 786440 | tf_op jit(solution)/shard_map/ppermute | solution.py:33
  56.5 14.7 %collective-permute-start.13 = (bf16[2,256,256]{2,1,0:T(8,128)(2,1)S(1)}, bf16[2,256,256]{2,1,0:T(8,128)(2,1)S(1)}, u32[]{:S(2)}, u32[]{:S(2)}) collective-permute-start(bf16[2,256,256]{2,1,0:T(8,128)(2,1)S(1)} %get-tuple-element.56), channel_id=1, source_target_pairs={{0,192},{64,0},{128,64},{192,128},{1,193},{65,1},{129,65},{193,129... | collective-permute-start | bytes 786440 | tf_op jit(solution)/shard_map/ppermute | solution.py:33
  60.2 11.0 %collective-permute-start.15 = (bf16[2,256,256]{2,1,0:T(8,128)(2,1)S(1)}, bf16[2,256,256]{2,1,0:T(8,128)(2,1)S(1)}, u32[]{:S(2)}, u32[]{:S(2)}) collective-permute-start(bf16[2,256,256]{2,1,0:T(8,128)(2,1)S(1)} %add_convert_fusion), channel_id=1, source_target_pairs={{0,63},{1,0},{2,1},{3,2},{4,3},{5,4},{6,5},{7,6},{8,7},{9,8},{10,9... | collective-permute-start | bytes 786440 | tf_op jit(solution)/shard_map/ppermute | solution.py:33
  65.2 8.4 %collective-permute-start.6 = (bf16[2,256,256]{2,1,0:T(8,128)(2,1)S(1)}, bf16[2,256,256]{2,1,0:T(8,128)(2,1)S(1)}, u32[]{:S(2)}, u32[]{:S(2)}) collective-permute-start(bf16[2,256,256]{2,1,0:T(8,128)(2,1)S(1)} %add2.1), channel_id=1, source_target_pairs={{0,192},{64,0},{128,64},{192,128},{1,193},{65,1},{129,65},{193,129... | collective-permute-start | bytes 786440 | tf_op jit(solution)/shard_map/ppermute | solution.py:33
  66.5 10.7 %collective-permute-start.10 = (bf16[2,256,256]{2,1,0:T(8,128)(2,1)S(1)}, bf16[2,256,256]{2,1,0:T(8,128)(2,1)S(1)}, u32[]{:S(2)}, u32[]{:S(2)}) collective-permute-start(bf16[2,256,256]{2,1,0:T(8,128)(2,1)S(1)} %below2.1), channel_id=1, source_target_pairs={{0,63},{1,0},{2,1},{3,2},{4,3},{5,4},{6,5},{7,6},{8,7},{9,8},{10,9... | collective-permute-start | bytes 786440 | tf_op jit(solution)/shard_map/ppermute | solution.py:33
